TPU v7x, 512 devices: a whole 4x4x16 slice. The times are simulated.
512 devices in a mesh: dp: 8 (over z_hi, core), frames: 4 (over x), rows: 16 (over y, z_lo).
Axes of the slice: x: 4, y: 4, z: 16 (z_hi: 4, z_lo: 4; z = z_hi * 4 + z_lo), core: 2. Of those that a mesh axis runs over, the one named last changes fastest.
Arguments:
- acts_fine: bfloat16 [8, 8, 64, 16, 512], P('dp', 'frames', 'rows'), may hold values from -120 to 120
- acts_coarse: bfloat16 [8, 8, 32, 8, 512], P('dp', 'frames', 'rows'), may hold values from -120 to 120
- grad_coarse: bfloat16 [8, 8, 32, 8, 512], P('dp', 'frames', 'rows'), may hold values from -20 to 20
- gain_fine: float32 [512], replicated, may hold values from 0.5 to 1.5
- bias_fine: float32 [512], replicated, may hold values from -1 to 1
- kernel_fine: bfloat16 [27, 512, 512], P(None, 'rows'), may hold values from -0.0546875 to 0.0546875
- gain_coarse: float32 [512], replicated, may hold values from 0.5 to 1.5
- bias_coarse: float32 [512], replicated, may hold values from -1 to 1
- kernel_coarse: bfloat16 [27, 512, 512], P(None, 'rows'), may hold values from -0.0546875 to 0.0546875
Outputs:
- grad_fine: bfloat16 [8, 8, 64, 16, 512], P('dp', 'frames', 'rows')
- gain_grad_fine: float32 [512], replicated
- bias_grad_fine: float32 [512], replicated
- gain_grad_coarse: float32 [512], replicated
- bias_grad_coarse: float32 [512], replicated
All inputs are finite; a program needn't handle non-finite values.
Results may differ from a plain program's by a relative error of at most 0.0048.
Values may be sent and summed in bfloat16 or wider, within the bound.
A program may use at most 64 MiB of HBM per device.

v0:
```python
import functools

import jax
import jax.numpy as jnp
from jax import lax
from jax.experimental import pallas as pl
from jax.experimental.pallas import tpu as pltpu
from jax.sharding import PartitionSpec as P

GROUPS = 32
EPSILON = 1e-06
MESH = pl.DeviceIdType.MESH
LANES = 128


def iota(shape, dim):
    return lax.broadcasted_iota(jnp.int32, shape, dim)


def one_hot(cond, dtype=jnp.bfloat16):
    return jnp.where(cond, 1.0, 0.0).astype(dtype)


def fine_position(new):
    frame, p, q, a, b = new >> 6, (new >> 5) & 1, (new >> 4) & 1, (new >> 3) & 1, new & 7
    return frame * 64 + (2 * a + p) * 16 + 2 * b + q


def chunk_swap(arrays, chunk):
    arrays = list(arrays)
    for bit in range(3):
        step = 1 << bit
        low = ((chunk >> bit) & 1) == 0
        for i in range(8):
            if i & step:
                continue
            one, two = arrays[i], arrays[i + step]
            arrays[i] = jnp.where(low, one, pltpu.roll(two, 16 * step, 1))
            arrays[i + step] = jnp.where(low, pltpu.roll(one, LANES - 16 * step, 1), two)
    return arrays


def group_total(column):
    per_group = column.shape[0] // 2
    split = column.reshape(2, per_group, 1)
    return jnp.broadcast_to(jnp.sum(split, axis=1, keepdims=True), split.shape).reshape(column.shape)


def columns_of(parts, lane):
    block = jnp.zeros(lane.shape, jnp.float32)
    for k, part in enumerate(parts):
        block = jnp.where(lane == k, part, block)
    return block


def row_sum(x):
    return jnp.sum(x, axis=1, keepdims=True)


def kernel(
    sizes,
    acts_fine,
    acts_coarse,
    grad_coarse,
    gain_fine,
    bias_fine,
    gain_coarse,
    bias_coarse,
    kernel_fine,
    kernel_coarse,
    out,
    par,
    weights_f,
    weights_c,
    sent_f,
    sent_c,
    got_f,
    got_c,
    cot,
    quart,
    prod,
    halo_out_c,
    halo_in_c,
    halo_out_f,
    halo_in_f,
    stats,
    par_dp,
    par_rows,
    grad_out,
    grad_in,
    load_sem,
    send_rows,
    recv_rows,
    send_frames,
    recv_frames,
    send_halo,
    recv_halo,
    send_dp,
    recv_dp,
):
    n_dp, n_frames, n_rows = sizes
    dp, fr, row = lax.axis_index("dp"), lax.axis_index("frames"), lax.axis_index("rows")
    width = weights_f.shape[0] // 27

    loads = [
        pltpu.make_async_copy(kernel_coarse, weights_c, load_sem.at[0]),
        pltpu.make_async_copy(kernel_fine, weights_f, load_sem.at[1]),
    ]
    for load in loads:
        load.start()

    barrier = pltpu.get_barrier_semaphore()
    for axis, me, count in (("rows", row, n_rows), ("frames", fr, n_frames), ("dp", dp, n_dp)):

        def greet(d, carry, axis=axis, me=me, count=count):
            pl.semaphore_signal(barrier, inc=1, device_id={axis: lax.rem(me + d, count)}, device_id_type=MESH)
            return carry

        if count > 1:
            lax.fori_loop(1, count, greet, 0)

    new, old = iota((LANES, LANES), 0), iota((LANES, LANES), 1)
    to_new = one_hot(old == fine_position(new))
    to_old = one_hot(new == fine_position(old))
    moved = jnp.dot(to_new, acts_fine[...], preferred_element_type=jnp.float32)
    sent_f[...] = moved.T.astype(jnp.bfloat16)
    place, source = iota((LANES, 32), 0), iota((LANES, 32), 1)
    eighth = lax.rem(row, 8)
    at_first = ((place >> 4) == eighth) & (source == (place & 15))
    at_second = ((place >> 4) == lax.rem(eighth + 4, 8)) & (source == 16 + (place & 15))
    placed = jnp.dot(one_hot(at_first | at_second), acts_coarse[...], preferred_element_type=jnp.float32)
    sent_c[...] = placed.T.astype(jnp.bfloat16)

    pl.semaphore_wait(barrier, (n_rows - 1) + (n_frames - 1) + (n_dp - 1))

    def slices(ref, index):
        return ref.at[pl.ds(pl.multiple_of(index * width, width), width)]

    def rows_copy(stage, target, source):
        if stage == 0:
            src, dst = grad_coarse, cot.at[:, source]
        elif stage == 1:
            src, dst = slices(sent_c, target), got_c.at[source]
        elif stage == 2:
            src, dst = slices(sent_f, target), got_f.at[source]
        elif stage == 3:
            src, dst = quart.at[row], quart.at[source]
        elif stage == 4:
            src, dst = grad_out.at[target], grad_in.at[source]
        else:
            src, dst = par_rows.at[row], par_rows.at[source]
        return pltpu.make_async_remote_copy(
            src_ref=src,
            dst_ref=dst,
            send_sem=send_rows.at[stage, target],
            recv_sem=recv_rows.at[stage, source],
            device_id={"rows": target},
            device_id_type=MESH,
        )

    def rows_send(stage):
        def step(d, carry):
            rows_copy(stage, lax.rem(row + d, n_rows), row).start()
            return carry

        lax.fori_loop(1, n_rows, step, 0)

    def rows_wait(stage):
        def step(d, carry):
            other = lax.rem(row + n_rows - d, n_rows)
            rows_copy(stage, other, other).wait_recv()
            return carry

        lax.fori_loop(1, n_rows, step, 0)

    def rows_sent(stage):
        def step(d, carry):
            rows_copy(stage, lax.rem(row + d, n_rows), row).wait_send()
            return carry

        lax.fori_loop(1, n_rows, step, 0)

    def frames_copy(stage, target, source):
        return pltpu.make_async_remote_copy(
            src_ref=stats.at[stage, fr],
            dst_ref=stats.at[stage, source],
            send_sem=send_frames.at[stage, target],
            recv_sem=recv_frames.at[stage, source],
            device_id={"frames": target},
            device_id_type=MESH,
        )

    def frames_start(stage, block):
        stats[stage, fr] = block

        def step(d, carry):
            frames_copy(stage, lax.rem(fr + d, n_frames), fr).start()
            return carry

        lax.fori_loop(1, n_frames, step, 0)

    def frames_total(stage):
        def step(d, carry):
            other = lax.rem(fr + n_frames - d, n_frames)
            frames_copy(stage, other, other).wait_recv()
            return carry

        lax.fori_loop(1, n_frames, step, 0)
        total = stats[stage, 0]
        for k in range(1, n_frames):
            total = total + stats[stage, k]
        return total

    def halo_copy(stage):
        src, dst = ((halo_out_c, halo_in_c), (halo_out_f, halo_in_f))[stage]
        return pltpu.make_async_remote_copy(
            src_ref=src,
            dst_ref=dst,
            send_sem=send_halo.at[stage],
            recv_sem=recv_halo.at[stage],
            device_id={"frames": lax.rem(fr + n_frames - 1, n_frames)},
            device_id_type=MESH,
        )

    def halo_send(stage):
        @pl.when(fr > 0)
        def _():
            halo_copy(stage).start()

    def halo_wait(stage):
        @pl.when(fr < n_frames - 1)
        def _():
            halo_copy(stage).wait_recv()

        @pl.when(fr == n_frames - 1)
        def _():
            into = (halo_in_c, halo_in_f)[stage]
            into[...] = jnp.zeros_like(into)

    own = pltpu.make_async_copy(grad_coarse, cot.at[:, row], load_sem.at[2])
    own.start()
    rows_send(0)
    rows_send(1)
    rows_send(2)
    got_c[row] = sent_c[pl.ds(pl.multiple_of(row * width, width), width), :]
    got_f[row] = sent_f[pl.ds(pl.multiple_of(row * width, width), width), :]

    wide = iota((width, gain_fine.shape[1]), 1) == row * width + iota((width, gain_fine.shape[1]), 0)

    def column(vector):
        return row_sum(jnp.where(wide, vector[...], 0.0))

    gain_f, bias_f, gain_c, bias_c = (column(v) for v in (gain_fine, bias_fine, gain_coarse, bias_coarse))
    lane = iota((width, LANES), 1)
    chunk = lane >> 4

    cells = 256
    spot = iota((width, cells), 1)
    top, bottom = spot >= 8, spot < cells - 8
    left, right = (spot & 7) > 0, (spot & 7) < 7

    def above(x):
        return jnp.where(top, pltpu.roll(x, 8, 1), 0.0)

    def below(x):
        return jnp.where(bottom, pltpu.roll(x, cells - 8, 1), 0.0)

    def before(x):
        return jnp.where(left, pltpu.roll(x, 1, 1), 0.0)

    def after(x):
        return jnp.where(right, pltpu.roll(x, cells - 1, 1), 0.0)

    def product(depth, tap, frame):
        at = (depth * 9 + tap) * width
        return prod[at : at + width, frame * cells : (frame + 1) * cells]

    def spatial_taps(which):
        terms = (((0, 0),), ((1, 0), (0, 1)), ((2, 0), (1, 1)), ((2, 1),))[which]
        taps = []
        for tap in range(9):
            total = product(terms[0][0], tap, terms[0][1])
            for depth, frame in terms[1:]:
                total = total + product(depth, tap, frame)
            taps.append(total)
        return taps

    def coarse_frame(which):
        t = spatial_taps(which)
        r = [below(t[kw]) + t[3 + kw] + above(t[6 + kw]) for kw in range(3)]
        return after(r[0]) + r[1] + before(r[2])

    def fine_frame(which):
        t = spatial_taps(which)
        planes = []
        for p in range(2):
            if p == 0:
                r = [t[kw] + t[3 + kw] + above(t[6 + kw]) for kw in range(3)]
            else:
                r = [below(t[kw]) + t[3 + kw] + t[6 + kw] for kw in range(3)]
            planes.append(r[0] + r[1] + before(r[2]))
            planes.append(after(r[0]) + r[1] + r[2])
        return planes

    rows_wait(1)
    firsts, seconds = [], []
    for half in range(2):
        first = jnp.zeros((width, LANES), jnp.float32)
        second = jnp.zeros((width, LANES), jnp.float32)
        for j in range(8):
            block = got_c[8 * half + j].astype(jnp.float32)
            first = jnp.where(chunk == j, block, first)
            second = jnp.where(chunk == (j + 4) % 8, block, second)
        firsts.append(first)
        seconds.append(pltpu.roll(second, 64, 1))
    values_c = jnp.concatenate(firsts + seconds, axis=1)
    rows_wait(2)
    swapped = []
    for half in range(2):
        swapped.append(chunk_swap([got_f[8 * half + j].astype(jnp.float32) for j in range(8)], chunk))
    values_f = jnp.concatenate([swapped[half][c] for c in range(8) for half in range(2)], axis=1)
    frames_start(
        0,
        columns_of(
            (row_sum(values_f), row_sum(values_f * values_f), row_sum(values_c), row_sum(values_c * values_c)), lane
        ),
    )

    loads[0].wait()
    own.wait()
    rows_wait(0)
    gathered = cot[...].reshape(2 * n_rows * 16, cot.shape[3])
    nt = (((1,), (1,)), ((), ()))
    prod[...] = lax.dot_general(weights_c[...], gathered, nt, preferred_element_type=jnp.float32)
    halo_out_c[:, 0:cells] = coarse_frame(0)
    halo_out_c[:, cells:] = coarse_frame(1)
    halo_send(0)
    conv_c = jnp.concatenate([coarse_frame(2), coarse_frame(3)], axis=1)
    picked = one_hot(wide)
    cot_c = lax.dot_general(picked, gathered, nt, preferred_element_type=jnp.float32)

    entries_c = 16 * 2 * n_frames * cells
    entries_f = 4 * entries_c
    moments = frames_total(0)

    def norm_of(at, entries):
        mean = group_total(moments[:, at : at + 1]) / entries
        square = group_total(moments[:, at + 1 : at + 2]) / entries
        return mean, lax.rsqrt(square - mean * mean + EPSILON)

    def through(values, gain, bias, mean, inv):
        normed = (values - mean) * inv
        pre = gain * normed + bias
        squash = jax.nn.sigmoid(pre)
        return normed, squash * (1.0 + pre * (1.0 - squash))

    mean_c, inv_c = norm_of(2, entries_c)
    mean_f, inv_f = norm_of(0, entries_f)
    normed_c, slope_c = through(values_c, gain_c, bias_c, mean_c, inv_c)

    halo_wait(0)
    pre_grad_c = (conv_c + halo_in_c[...]) * slope_c
    frames_start(1, columns_of((row_sum(pre_grad_c), row_sum(pre_grad_c * normed_c)), lane))
    totals_c = frames_total(1)
    one_c, two_c = totals_c[:, 0:1], totals_c[:, 1:2]

    def level(cot, normed, pre_grad, gain, inv, one, two, entries):
        group_one = group_total(gain * one) / entries
        group_two = group_total(gain * two) / entries
        return cot + inv * (gain * pre_grad - group_one - normed * group_two)

    level_c = level(cot_c, normed_c, pre_grad_c, gain_c, inv_c, one_c, two_c, entries_c)
    quarter = (level_c * 0.25).astype(jnp.bfloat16)
    quart[row] = quarter
    rows_send(3)

    normed_f, slope_f = through(values_f, gain_f, bias_f, mean_f, inv_f)
    loads[1].wait()
    rows_wait(3)
    prod[...] = jnp.dot(
        weights_f[...], quart[...].reshape(n_rows * width, 2 * cells), preferred_element_type=jnp.float32
    )
    for which in range(2):
        halo_out_f[:, which * 4 * cells : (which + 1) * 4 * cells] = jnp.concatenate(
            fine_frame(which), axis=1
        ).astype(halo_out_f.dtype)
    halo_send(1)
    conv_f = jnp.concatenate(fine_frame(2) + fine_frame(3), axis=1)
    halo_wait(1)
    pre_grad_f = (conv_f + halo_in_f[...].astype(jnp.float32)) * slope_f
    frames_start(2, columns_of((row_sum(pre_grad_f), row_sum(pre_grad_f * normed_f)), lane))
    totals_f = frames_total(2)
    one_f, two_f = totals_f[:, 0:1], totals_f[:, 1:2]

    spread = lane == lax.rem(row, 4) * width + iota((width, LANES), 0)
    which_row = iota((8, LANES), 0)
    mine = jnp.zeros((8, LANES), jnp.float32)
    cells_all = n_dp * 2 * n_frames * cells
    scale_c, scale_f = 1.0 / cells_all**0.5, 1.0 / (4 * cells_all) ** 0.5
    for k, (sums, scale) in enumerate(((two_f, scale_f), (one_f, scale_f), (two_c, scale_c), (one_c, scale_c))):
        line = jnp.sum(jnp.where(spread, sums, 0.0), axis=0, keepdims=True) * scale
        mine = jnp.where(which_row == k, line, mine)
    par_dp[dp] = mine

    def dp_copy(target, source):
        return pltpu.make_async_remote_copy(
            src_ref=par_dp.at[dp],
            dst_ref=par_dp.at[source],
            send_sem=send_dp.at[target],
            recv_sem=recv_dp.at[source],
            device_id={"dp": target},
            device_id_type=MESH,
        )

    def dp_start(d, carry):
        dp_copy(lax.rem(dp + d, n_dp), dp).start()
        return carry

    def dp_wait(d, carry):
        other = lax.rem(dp + n_dp - d, n_dp)
        dp_copy(other, other).wait_recv()
        return carry

    def dp_sent(d, carry):
        dp_copy(lax.rem(dp + d, n_dp), dp).wait_send()
        return carry

    if n_dp > 1:
        lax.fori_loop(1, n_dp, dp_start, 0)

    four = [quarter[:, frame * cells : (frame + 1) * cells].astype(jnp.float32) for frame in range(2)]
    cot_f = jnp.concatenate([four[c // 4] for c in range(8)], axis=1)
    level_f = level(cot_f, normed_f, pre_grad_f, gain_f, inv_f, one_f, two_f, entries_f)
    for half in range(2):
        planes = [level_f[:, c * cells + half * LANES : c * cells + (half + 1) * LANES] for c in range(8)]
        for j, block in enumerate(chunk_swap(planes, chunk)):
            grad_out[8 * half + j] = block.astype(jnp.bfloat16)
    rows_send(4)
    grad_in[row] = grad_out[row]

    if n_dp > 1:
        lax.fori_loop(1, n_dp, dp_wait, 0)
    total = par_dp[0]
    for k in range(1, n_dp):
        total = total + par_dp[k]
    par_rows[row] = total
    rows_send(5)

    rows_wait(4)
    back = grad_in[...].reshape(n_rows * width, LANES).astype(jnp.float32).T.astype(jnp.bfloat16)
    out[...] = jnp.dot(to_old, back, preferred_element_type=jnp.float32).astype(out.dtype)

    rows_wait(5)
    for c in range(par.shape[1] // LANES):
        total = par_rows[4 * c]
        for k in range(1, 4):
            total = total + par_rows[4 * c + k]
        par[:, c * LANES : (c + 1) * LANES] = total

    for stage in range(6):
        rows_sent(stage)
    for stage in range(3):

        def frames_sent(d, carry, stage=stage):
            frames_copy(stage, lax.rem(fr + d, n_frames), fr).wait_send()
            return carry

        lax.fori_loop(1, n_frames, frames_sent, 0)

    @pl.when(fr > 0)
    def _():
        halo_copy(0).wait_send()
        halo_copy(1).wait_send()

    if n_dp > 1:
        lax.fori_loop(1, n_dp, dp_sent, 0)


def shards(
    sizes,
    acts_fine,
    acts_coarse,
    grad_coarse,
    gain_fine,
    bias_fine,
    kernel_fine,
    gain_coarse,
    bias_coarse,
    kernel_coarse,
):
    n_dp, n_frames, n_rows = sizes
    channels = acts_fine.shape[-1]
    width = channels // n_rows
    positions = 2 * n_rows * 16
    bf16, f32 = jnp.bfloat16, jnp.float32
    vmem = pl.BlockSpec(memory_space=pltpu.VMEM)
    anywhere = pl.BlockSpec(memory_space=pl.ANY)
    dma = pltpu.SemaphoreType.DMA
    taps = kernel_fine.shape[0]
    out, par = pl.pallas_call(
        functools.partial(kernel, sizes),
        out_shape=(
            jax.ShapeDtypeStruct((LANES, channels), bf16),
            jax.ShapeDtypeStruct((8, channels), f32),
        ),
        in_specs=[vmem] * 7 + [anywhere] * 2,
        out_specs=(vmem, vmem),
        scratch_shapes=[
            pltpu.VMEM((taps * width, channels), bf16),
            pltpu.VMEM((taps * width, channels), bf16),
            pltpu.VMEM((channels, LANES), bf16),
            pltpu.VMEM((channels, LANES), bf16),
            pltpu.VMEM((n_rows, width, LANES), bf16),
            pltpu.VMEM((n_rows, width, LANES), bf16),
            pltpu.VMEM((2, n_rows, 16, channels), bf16),
            pltpu.VMEM((n_rows, width, positions), bf16),
            pltpu.VMEM((taps * width, positions), f32),
            pltpu.VMEM((width, positions), f32),
            pltpu.VMEM((width, positions), f32),
            pltpu.VMEM((width, 4 * positions), bf16),
            pltpu.VMEM((width, 4 * positions), bf16),
            pltpu.VMEM((3, n_frames, width, LANES), f32),
            pltpu.VMEM((n_dp, 8, LANES), f32),
            pltpu.VMEM((n_rows, 8, LANES), f32),
            pltpu.VMEM((n_rows, width, LANES), bf16),
            pltpu.VMEM((n_rows, width, LANES), bf16),
            dma((3,)),
            dma((6, n_rows)),
            dma((6, n_rows)),
            dma((3, n_frames)),
            dma((3, n_frames)),
            dma((2,)),
            dma((2,)),
            dma((n_dp,)),
            dma((n_dp,)),
        ],
        compiler_params=pltpu.CompilerParams(collective_id=0, has_side_effects=True),
        name="levels",
    )(
        acts_fine.reshape(LANES, channels),
        acts_coarse.reshape(32, channels),
        grad_coarse.reshape(2, 16, channels),
        gain_fine.reshape(1, channels),
        bias_fine.reshape(1, channels),
        gain_coarse.reshape(1, channels),
        bias_coarse.reshape(1, channels),
        kernel_fine.reshape(taps * width, channels),
        kernel_coarse.reshape(taps * width, channels),
    )
    return (out.reshape(acts_fine.shape), par[0], par[1], par[2], par[3])


def solution(mesh):
    sizes = (mesh.shape["dp"], mesh.shape["frames"], mesh.shape["rows"])
    tall = P("dp", "frames", "rows", None, None)
    in_specs = (tall, tall, tall, P(), P(), P(None, "rows", None), P(), P(), P(None, "rows", None))
    out_specs = (tall, P(), P(), P(), P())
    return jax.shard_map(
        functools.partial(shards, sizes), mesh=mesh, in_specs=in_specs, out_specs=out_specs, check_vma=False
    )
```

profile of v0, /device:TPU:1, one launch (start us, length us, event | category | flops | bytes accessed | tf_op | source)
XLA Modules:
  0.0 85.2 jit_solution(6004145012762547230)
XLA Ops:
  0.6 81.6 %levels.1 = (bf16[128,512]{1,0:T(8,128)(2,1)}, f32[8,512]{1,0:T(8,128)}) custom-call(bf16[128,512]{1,0:T(8,128)(2,1)} %bitcast.17, bf16[32,512]{1,0:T(8,128)(2,1)} %bitcast.18, bf16[2,16,512]{2,1,0:T(8,128)(2,1)} %bitcast.19, f32[1,512]{1,0:T(1,128)} %bitcast.24, f32[1,512]{1,0:T(1,128)} %bitcast.25, f32[1,512]{1,0:T(1,128)} %bitcast.26, f32[1,512]{1,0:T(1,128)} %bitcast.27, ...), custom_call_target="tpu_custom_call" | custom-call | tf_op jit(solution)/shard_map/levels/pallas_call | solution.py:500
  82.2 1.5 %fusion = (f32[1,512]{1,0:T(1,128)}, f32[1,512]{1,0:T(1,128)}, f32[1,512]{1,0:T(1,128)}, f32[1,512]{1,0:T(1,128)}) fusion(f32[8,512]{1,0:T(8,128)} %get-tuple-element.8), kind=kLoop, calls=%fused_computation | loop fusion | bytes 16384 | tf_op jit(solution)/shard_map/slice | solution.py:550
  83.7 1.6 %copy.15 = bf16[1,2,4,16,512]{4,3,2,1,0:T(8,128)(2,1)} copy(bf16[1,2,4,16,512]{4,3,2,1,0:T(8,128)(2,1)} %bitcast.16) | data formatting | bytes 262144
where the time goes:
time: 85.5 us; the launch traced here: 85.2 us
  Pallas kernels  81.6 us (95%)
  local copies, waits for them, and re-layouts  3.03 us (4%)
    pallas_call x1, Pallas kernels, shards(): pl.pallas_call(functools.partial(kernel, sizes), out_shape=(jax.ShapeDtyp...  81.6 us

commit v1 on v0

--- a/solution.py
+++ b/solution.py
@@ -46,11 +46,15 @@
     return jnp.broadcast_to(jnp.sum(split, axis=1, keepdims=True), split.shape).reshape(column.shape)
 
 
-def columns_of(parts, lane):
-    block = jnp.zeros(lane.shape, jnp.float32)
-    for k, part in enumerate(parts):
-        block = jnp.where(lane == k, part, block)
-    return block
+def row_of(columns, diagonal):
+    spread = jnp.zeros(diagonal.shape, jnp.float32)
+    for k, column in enumerate(columns):
+        spread = jnp.where(diagonal == k, column, spread)
+    return jnp.sum(spread, axis=0, keepdims=True)
+
+
+def column_of(row, diagonal, k):
+    return row_sum(jnp.where(diagonal == k, row, 0.0))
 
 
 def row_sum(x):
@@ -97,6 +101,9 @@
     recv_halo,
     send_dp,
     recv_dp,
+    send_relay,
+    recv_relay,
+    ready,
 ):
     n_dp, n_frames, n_rows = sizes
     dp, fr, row = lax.axis_index("dp"), lax.axis_index("frames"), lax.axis_index("rows")
@@ -109,15 +116,21 @@
     for load in loads:
         load.start()
 
+    even = dp + 1 - 2 * lax.rem(dp, 2)
+    ring = [lax.rem(dp + step, n_dp) for step in (2, n_dp - 2)] if n_dp == 8 else []
+    near_dp = [even] + ring + [lax.rem(even + step, n_dp) for step in (2, n_dp - 2)] if n_dp == 8 else []
     barrier = pltpu.get_barrier_semaphore()
-    for axis, me, count in (("rows", row, n_rows), ("frames", fr, n_frames), ("dp", dp, n_dp)):
+    for axis, me, count in (("rows", row, n_rows), ("frames", fr, n_frames)):
 
         def greet(d, carry, axis=axis, me=me, count=count):
             pl.semaphore_signal(barrier, inc=1, device_id={axis: lax.rem(me + d, count)}, device_id_type=MESH)
             return carry
 
-        if count > 1:
-            lax.fori_loop(1, count, greet, 0)
+        lax.fori_loop(1, count, greet, 0)
+    for peer in near_dp:
+        pl.semaphore_signal(barrier, inc=1, device_id={"dp": peer}, device_id_type=MESH)
+
+    cot[:, row] = grad_coarse[...]
 
     new, old = iota((LANES, LANES), 0), iota((LANES, LANES), 1)
     to_new = one_hot(old == fine_position(new))
@@ -125,27 +138,27 @@
     moved = jnp.dot(to_new, acts_fine[...], preferred_element_type=jnp.float32)
     sent_f[...] = moved.T.astype(jnp.bfloat16)
     place, source = iota((LANES, 32), 0), iota((LANES, 32), 1)
-    eighth = lax.rem(row, 8)
-    at_first = ((place >> 4) == eighth) & (source == (place & 15))
-    at_second = ((place >> 4) == lax.rem(eighth + 4, 8)) & (source == 16 + (place & 15))
-    placed = jnp.dot(one_hot(at_first | at_second), acts_coarse[...], preferred_element_type=jnp.float32)
-    sent_c[...] = placed.T.astype(jnp.bfloat16)
-
-    pl.semaphore_wait(barrier, (n_rows - 1) + (n_frames - 1) + (n_dp - 1))
+    placed = jnp.dot(one_hot((place & 31) == source), acts_coarse[...], preferred_element_type=jnp.float32)
+    quads = placed.T.reshape(n_rows, 4, 8, LANES)
+    quad = iota((n_rows, 8, LANES), 2) >> 5
+    folded = jnp.where(quad == 0, quads[:, 0], 0.0)
+    for k in range(1, 4):
+        folded = jnp.where(quad == k, quads[:, k], folded)
+    sent_c[...] = folded.astype(jnp.bfloat16)
+
+    pl.semaphore_wait(barrier, (n_rows - 1) + (n_frames - 1) + len(near_dp))
+    for peer in ring:
+        pl.semaphore_signal(ready, inc=1, device_id={"dp": peer}, device_id_type=MESH)
 
     def slices(ref, index):
         return ref.at[pl.ds(pl.multiple_of(index * width, width), width)]
 
     def rows_copy(stage, target, source):
         if stage == 0:
-            src, dst = grad_coarse, cot.at[:, source]
+            src, dst = sent_c.at[target], got_c.at[source]
         elif stage == 1:
-            src, dst = slices(sent_c, target), got_c.at[source]
+            src, dst = slices(sent_f, target), got_f.at[source]
         elif stage == 2:
-            src, dst = slices(sent_f, target), got_f.at[source]
-        elif stage == 3:
-            src, dst = quart.at[row], quart.at[source]
-        elif stage == 4:
             src, dst = grad_out.at[target], grad_in.at[source]
         else:
             src, dst = par_rows.at[row], par_rows.at[source]
@@ -158,6 +171,63 @@
             device_id_type=MESH,
         )
 
+    y, z = lax.div(row, 4), lax.rem(row, 4)
+    z_mate = (z, z + 1 - 2 * lax.rem(z, 2), lax.rem(z + 2, 4), 3 - z)
+    y_up, y_down, y_far = lax.rem(y + 1, 4), lax.rem(y + 3, 4), lax.rem(y + 2, 4)
+
+    def at(y_of, z_of):
+        return 4 * y_of + z_of
+
+    def relay(stage, k, slot, target):
+        block = (cot.at[:, slot], quart.at[slot])[stage]
+        return pltpu.make_async_remote_copy(
+            src_ref=block,
+            dst_ref=block,
+            send_sem=send_relay.at[stage, k],
+            recv_sem=recv_relay.at[stage, slot],
+            device_id={"rows": target},
+            device_id_type=MESH,
+        )
+
+    up, down = at(y_up, z), at(y_down, z)
+
+    def routes():
+        own = (None, row, [at(y, z_mate[1]), up, down, at(y, z_mate[2]), at(y, z_mate[3])])
+        return [
+            own,
+            (0, at(y, z_mate[1]), [up, down]),
+            (0, at(y_down, z_mate[0]), [up]),
+            (0, at(y, z_mate[2]), [up, down]),
+            (0, at(y_up, z_mate[1]), [down]),
+            (0, at(y, z_mate[3]), [up, down]),
+            (0, at(y_down, z_mate[2]), [up]),
+            (0, at(y_up, z_mate[3]), [down]),
+            (0, at(y_down, z_mate[1]), []),
+            (0, at(y_down, z_mate[3]), []),
+            (0, at(y_up, z_mate[0]), []),
+            (0, at(y_up, z_mate[2]), []),
+            (0, at(y_far, z_mate[0]), []),
+            (0, at(y_far, z_mate[1]), []),
+            (0, at(y_far, z_mate[2]), []),
+            (0, at(y_far, z_mate[3]), []),
+        ]
+
+    def gather_start(stage):
+        for k, target in enumerate(routes()[0][2]):
+            relay(stage, k, row, target).start()
+
+    def gather_finish(stage):
+        k = 5
+        for _, slot, targets in routes()[1:]:
+            relay(stage, 0, slot, row).wait_recv()
+            for target in targets:
+                relay(stage, k, slot, target).start()
+                k += 1
+
+    def gather_sent(stage):
+        for k in range(15):
+            relay(stage, k, row, up).wait_send()
+
     def rows_send(stage):
         def step(d, carry):
             rows_copy(stage, lax.rem(row + d, n_rows), row).start()
@@ -237,13 +307,9 @@
             into = (halo_in_c, halo_in_f)[stage]
             into[...] = jnp.zeros_like(into)
 
-    own = pltpu.make_async_copy(grad_coarse, cot.at[:, row], load_sem.at[2])
-    own.start()
+    gather_start(0)
     rows_send(0)
-    rows_send(1)
-    rows_send(2)
-    got_c[row] = sent_c[pl.ds(pl.multiple_of(row * width, width), width), :]
-    got_f[row] = sent_f[pl.ds(pl.multiple_of(row * width, width), width), :]
+    got_c[row] = sent_c[row]
 
     wide = iota((width, gain_fine.shape[1]), 1) == row * width + iota((width, gain_fine.shape[1]), 0)
 
@@ -251,8 +317,9 @@
         return row_sum(jnp.where(wide, vector[...], 0.0))
 
     gain_f, bias_f, gain_c, bias_c = (column(v) for v in (gain_fine, bias_fine, gain_coarse, bias_coarse))
-    lane = iota((width, LANES), 1)
+    lane, channel = iota((width, LANES), 1), iota((width, LANES), 0)
     chunk = lane >> 4
+    diagonal = jnp.where((lane & 31) == channel, lane >> 5, -1)
 
     cells = 256
     spot = iota((width, cells), 1)
@@ -302,38 +369,28 @@
             planes.append(after(r[0]) + r[1] + r[2])
         return planes
 
-    rows_wait(1)
-    firsts, seconds = [], []
-    for half in range(2):
-        first = jnp.zeros((width, LANES), jnp.float32)
-        second = jnp.zeros((width, LANES), jnp.float32)
-        for j in range(8):
-            block = got_c[8 * half + j].astype(jnp.float32)
-            first = jnp.where(chunk == j, block, first)
-            second = jnp.where(chunk == (j + 4) % 8, block, second)
-        firsts.append(first)
-        seconds.append(pltpu.roll(second, 64, 1))
-    values_c = jnp.concatenate(firsts + seconds, axis=1)
-    rows_wait(2)
-    swapped = []
-    for half in range(2):
-        swapped.append(chunk_swap([got_f[8 * half + j].astype(jnp.float32) for j in range(8)], chunk))
-    values_f = jnp.concatenate([swapped[half][c] for c in range(8) for half in range(2)], axis=1)
-    frames_start(
-        0,
-        columns_of(
-            (row_sum(values_f), row_sum(values_f * values_f), row_sum(values_c), row_sum(values_c * values_c)), lane
-        ),
+    gather_finish(0)
+
+    rows_wait(0)
+    pieces = [chunk_swap([got_c[8 * half + j].astype(jnp.float32) for j in range(8)], chunk[:8]) for half in range(2)]
+    values_c = jnp.concatenate(
+        [
+            jnp.concatenate([pieces[half][2 * quarter + frame] for quarter in range(4)], axis=0)
+            for frame in range(2)
+            for half in range(2)
+        ],
+        axis=1,
     )
+    frames_start(0, row_of((row_sum(values_c), row_sum(values_c * values_c)), diagonal))
+    rows_send(1)
+    got_f[row] = sent_f[pl.ds(pl.multiple_of(row * width, width), width), :]
 
     loads[0].wait()
-    own.wait()
-    rows_wait(0)
     gathered = cot[...].reshape(2 * n_rows * 16, cot.shape[3])
     nt = (((1,), (1,)), ((), ()))
     prod[...] = lax.dot_general(weights_c[...], gathered, nt, preferred_element_type=jnp.float32)
-    halo_out_c[:, 0:cells] = coarse_frame(0)
-    halo_out_c[:, cells:] = coarse_frame(1)
+    halo_out_c[:, 0:cells] = coarse_frame(0).astype(halo_out_c.dtype)
+    halo_out_c[:, cells:] = coarse_frame(1).astype(halo_out_c.dtype)
     halo_send(0)
     conv_c = jnp.concatenate([coarse_frame(2), coarse_frame(3)], axis=1)
     picked = one_hot(wide)
@@ -341,11 +398,10 @@
 
     entries_c = 16 * 2 * n_frames * cells
     entries_f = 4 * entries_c
-    moments = frames_total(0)
-
-    def norm_of(at, entries):
-        mean = group_total(moments[:, at : at + 1]) / entries
-        square = group_total(moments[:, at + 1 : at + 2]) / entries
+
+    def norm_of(moments, entries):
+        mean = group_total(column_of(moments, diagonal, 0)) / entries
+        square = group_total(column_of(moments, diagonal, 1)) / entries
         return mean, lax.rsqrt(square - mean * mean + EPSILON)
 
     def through(values, gain, bias, mean, inv):
@@ -354,15 +410,14 @@
         squash = jax.nn.sigmoid(pre)
         return normed, squash * (1.0 + pre * (1.0 - squash))
 
-    mean_c, inv_c = norm_of(2, entries_c)
-    mean_f, inv_f = norm_of(0, entries_f)
+    mean_c, inv_c = norm_of(frames_total(0), entries_c)
     normed_c, slope_c = through(values_c, gain_c, bias_c, mean_c, inv_c)
 
     halo_wait(0)
-    pre_grad_c = (conv_c + halo_in_c[...]) * slope_c
-    frames_start(1, columns_of((row_sum(pre_grad_c), row_sum(pre_grad_c * normed_c)), lane))
+    pre_grad_c = (conv_c + halo_in_c[...].astype(jnp.float32)) * slope_c
+    frames_start(1, row_of((row_sum(pre_grad_c), row_sum(pre_grad_c * normed_c)), diagonal))
     totals_c = frames_total(1)
-    one_c, two_c = totals_c[:, 0:1], totals_c[:, 1:2]
+    one_c, two_c = column_of(totals_c, diagonal, 0), column_of(totals_c, diagonal, 1)
 
     def level(cot, normed, pre_grad, gain, inv, one, two, entries):
         group_one = group_total(gain * one) / entries
@@ -372,11 +427,17 @@
     level_c = level(cot_c, normed_c, pre_grad_c, gain_c, inv_c, one_c, two_c, entries_c)
     quarter = (level_c * 0.25).astype(jnp.bfloat16)
     quart[row] = quarter
-    rows_send(3)
-
-    normed_f, slope_f = through(values_f, gain_f, bias_f, mean_f, inv_f)
+    gather_start(1)
+
+    rows_wait(1)
+    swapped = []
+    for half in range(2):
+        swapped.append(chunk_swap([got_f[8 * half + j].astype(jnp.float32) for j in range(8)], chunk))
+    values_f = jnp.concatenate([swapped[half][c] for c in range(8) for half in range(2)], axis=1)
+    frames_start(2, row_of((row_sum(values_f), row_sum(values_f * values_f)), diagonal))
+    gather_finish(1)
+
     loads[1].wait()
-    rows_wait(3)
     prod[...] = jnp.dot(
         weights_f[...], quart[...].reshape(n_rows * width, 2 * cells), preferred_element_type=jnp.float32
     )
@@ -386,20 +447,17 @@
         ).astype(halo_out_f.dtype)
     halo_send(1)
     conv_f = jnp.concatenate(fine_frame(2) + fine_frame(3), axis=1)
+    mean_f, inv_f = norm_of(frames_total(2), entries_f)
+    normed_f, slope_f = through(values_f, gain_f, bias_f, mean_f, inv_f)
     halo_wait(1)
     pre_grad_f = (conv_f + halo_in_f[...].astype(jnp.float32)) * slope_f
-    frames_start(2, columns_of((row_sum(pre_grad_f), row_sum(pre_grad_f * normed_f)), lane))
-    totals_f = frames_total(2)
-    one_f, two_f = totals_f[:, 0:1], totals_f[:, 1:2]
-
-    spread = lane == lax.rem(row, 4) * width + iota((width, LANES), 0)
-    which_row = iota((8, LANES), 0)
-    mine = jnp.zeros((8, LANES), jnp.float32)
+    frames_start(3, row_of((row_sum(pre_grad_f), row_sum(pre_grad_f * normed_f)), diagonal))
+    totals_f = frames_total(3)
+    one_f, two_f = column_of(totals_f, diagonal, 0), column_of(totals_f, diagonal, 1)
+
     cells_all = n_dp * 2 * n_frames * cells
     scale_c, scale_f = 1.0 / cells_all**0.5, 1.0 / (4 * cells_all) ** 0.5
-    for k, (sums, scale) in enumerate(((two_f, scale_f), (one_f, scale_f), (two_c, scale_c), (one_c, scale_c))):
-        line = jnp.sum(jnp.where(spread, sums, 0.0), axis=0, keepdims=True) * scale
-        mine = jnp.where(which_row == k, line, mine)
+    mine = row_of((two_f * scale_f, one_f * scale_f, two_c * scale_c, one_c * scale_c), diagonal)
     par_dp[dp] = mine
 
     def dp_copy(target, source):
@@ -425,6 +483,8 @@
         dp_copy(lax.rem(dp + d, n_dp), dp).wait_send()
         return carry
 
+    if ring:
+        pl.semaphore_wait(ready, len(ring))
     if n_dp > 1:
         lax.fori_loop(1, n_dp, dp_start, 0)
 
@@ -435,7 +495,7 @@
         planes = [level_f[:, c * cells + half * LANES : c * cells + (half + 1) * LANES] for c in range(8)]
         for j, block in enumerate(chunk_swap(planes, chunk)):
             grad_out[8 * half + j] = block.astype(jnp.bfloat16)
-    rows_send(4)
+    rows_send(2)
     grad_in[row] = grad_out[row]
 
     if n_dp > 1:
@@ -444,22 +504,32 @@
     for k in range(1, n_dp):
         total = total + par_dp[k]
     par_rows[row] = total
-    rows_send(5)
-
-    rows_wait(4)
+    rows_send(3)
+
+    rows_wait(2)
     back = grad_in[...].reshape(n_rows * width, LANES).astype(jnp.float32).T.astype(jnp.bfloat16)
     out[...] = jnp.dot(to_old, back, preferred_element_type=jnp.float32).astype(out.dtype)
 
-    rows_wait(5)
-    for c in range(par.shape[1] // LANES):
-        total = par_rows[4 * c]
-        for k in range(1, 4):
-            total = total + par_rows[4 * c + k]
-        par[:, c * LANES : (c + 1) * LANES] = total
-
-    for stage in range(6):
+    rows_wait(3)
+    lines = [jnp.concatenate([par_rows[4 * k + j] for k in range(4)], axis=0) for j in range(4)]
+    part = iota(lines[0].shape, 1) >> 5
+    for bit in range(2):
+        step = 1 << bit
+        low = ((part >> bit) & 1) == 0
+        for i in range(4):
+            if i & step:
+                continue
+            one, two = lines[i], lines[i + step]
+            lines[i] = jnp.where(low, one, pltpu.roll(two, 32 * step, 1))
+            lines[i + step] = jnp.where(low, pltpu.roll(one, LANES - 32 * step, 1), two)
+    for k in range(4):
+        par[k] = lines[k]
+
+    gather_sent(0)
+    gather_sent(1)
+    for stage in range(4):
         rows_sent(stage)
-    for stage in range(3):
+    for stage in range(4):
 
         def frames_sent(d, carry, stage=stage):
             frames_copy(stage, lax.rem(fr + d, n_frames), fr).wait_send()
@@ -501,7 +571,7 @@
         functools.partial(kernel, sizes),
         out_shape=(
             jax.ShapeDtypeStruct((LANES, channels), bf16),
-            jax.ShapeDtypeStruct((8, channels), f32),
+            jax.ShapeDtypeStruct((4, channels // LANES, LANES), f32),
         ),
         in_specs=[vmem] * 7 + [anywhere] * 2,
         out_specs=(vmem, vmem),
@@ -509,30 +579,33 @@
             pltpu.VMEM((taps * width, channels), bf16),
             pltpu.VMEM((taps * width, channels), bf16),
             pltpu.VMEM((channels, LANES), bf16),
-            pltpu.VMEM((channels, LANES), bf16),
+            pltpu.VMEM((n_rows, 8, LANES), bf16),
             pltpu.VMEM((n_rows, width, LANES), bf16),
-            pltpu.VMEM((n_rows, width, LANES), bf16),
+            pltpu.VMEM((n_rows, 8, LANES), bf16),
             pltpu.VMEM((2, n_rows, 16, channels), bf16),
             pltpu.VMEM((n_rows, width, positions), bf16),
             pltpu.VMEM((taps * width, positions), f32),
-            pltpu.VMEM((width, positions), f32),
-            pltpu.VMEM((width, positions), f32),
+            pltpu.VMEM((width, positions), bf16),
+            pltpu.VMEM((width, positions), bf16),
             pltpu.VMEM((width, 4 * positions), bf16),
             pltpu.VMEM((width, 4 * positions), bf16),
-            pltpu.VMEM((3, n_frames, width, LANES), f32),
-            pltpu.VMEM((n_dp, 8, LANES), f32),
-            pltpu.VMEM((n_rows, 8, LANES), f32),
+            pltpu.VMEM((4, n_frames, 1, LANES), f32),
+            pltpu.VMEM((n_dp, 1, LANES), f32),
+            pltpu.VMEM((n_rows, 1, LANES), f32),
             pltpu.VMEM((n_rows, width, LANES), bf16),
             pltpu.VMEM((n_rows, width, LANES), bf16),
-            dma((3,)),
-            dma((6, n_rows)),
-            dma((6, n_rows)),
-            dma((3, n_frames)),
-            dma((3, n_frames)),
+            dma((2,)),
+            dma((4, n_rows)),
+            dma((4, n_rows)),
+            dma((4, n_frames)),
+            dma((4, n_frames)),
             dma((2,)),
             dma((2,)),
             dma((n_dp,)),
             dma((n_dp,)),
+            dma((2, 15)),
+            dma((2, n_rows)),
+            pltpu.SemaphoreType.REGULAR,
         ],
         compiler_params=pltpu.CompilerParams(collective_id=0, has_side_effects=True),
         name="levels",
@@ -547,7 +620,8 @@
         kernel_fine.reshape(taps * width, channels),
         kernel_coarse.reshape(taps * width, channels),
     )
-    return (out.reshape(acts_fine.shape), par[0], par[1], par[2], par[3])
+    vectors = par.reshape(4, channels)
+    return (out.reshape(acts_fine.shape), vectors[0], vectors[1], vectors[2], vectors[3])
 
 
 def solution(mesh):

time: 85.5 us -> 78.9 us (0.923)
  Pallas kernels: 81.6 us -> 75.3 us
    pallas_call x1, Pallas kernels: 81.6 us -> 75.3 us  [shards(): pl.pallas_call(functools.partial(kernel, sizes), out_shape=(jax.ShapeDtyp...]
    slice x1 -> x0, local copies, waits for them, and re-layouts: 1.46 us -> none  [shards(): return (out.reshape(acts_fine.shape), par[0], par[1], par[2], par[3])]
    squeeze x0 -> x1, local copies, waits for them, and re-layouts: none -> 1.29 us  [shards(): vectors[3]]
where the time goes in v1:
time: 78.9 us; the launch traced here: 78.7 us
  Pallas kernels  75.3 us (95%)
  local copies, waits for them, and re-layouts  2.85 us (4%)
    pallas_call x1, Pallas kernels, shards(): pl.pallas_call(functools.partial(kernel, sizes), out_shape=(jax.ShapeDtyp...  75.3 us

profile of v1, /device:TPU:1, one launch (start us, length us, event | category | flops | bytes accessed | tf_op | source)
XLA Modules:
  0.0 78.7 jit_solution(10560984379629168273)
XLA Ops:
  0.6 75.3 %levels.1 = (bf16[128,512]{1,0:T(8,128)(2,1)}, f32[4,4,128]{2,1,0:T(4,128)}) custom-call(bf16[128,512]{1,0:T(8,128)(2,1)} %bitcast.21, bf16[32,512]{1,0:T(8,128)(2,1)} %bitcast.22, bf16[2,16,512]{2,1,0:T(8,128)(2,1)} %bitcast.23, f32[1,512]{1,0:T(1,128)} %bitcast.24, f32[1,512]{1,0:T(1,128)} %bitcast.25, f32[1,512]{1,0:T(1,128)} %bitcast.26, ...), custom_call_target="tpu_custom_call" | custom-call | tf_op jit(solution)/shard_map/levels/pallas_call | solution.py:570
  75.9 1.3 %slice_bitcast_fusion = (f32[512]{0:T(512)}, f32[512]{0:T(512)}, f32[512]{0:T(512)}, f32[512]{0:T(512)}) fusion(f32[4,4,128]{2,1,0:T(4,128)} %get-tuple-element.8), kind=kLoop, calls=%fused_computation | loop fusion | bytes 16384 | tf_op jit(solution)/shard_map/squeeze | solution.py:624
  77.2 1.6 %copy.15 = bf16[1,2,4,16,512]{4,3,2,1,0:T(8,128)(2,1)} copy(bf16[1,2,4,16,512]{4,3,2,1,0:T(8,128)(2,1)} %bitcast.20) | data formatting | bytes 262144

commit v2 on v1

--- a/solution.py
+++ b/solution.py
@@ -63,17 +63,20 @@
 
 def kernel(
     sizes,
-    acts_fine,
-    acts_coarse,
-    grad_coarse,
-    gain_fine,
-    bias_fine,
-    gain_coarse,
-    bias_coarse,
+    acts_fine_hbm,
+    acts_coarse_hbm,
+    grad_coarse_hbm,
+    gain_fine_hbm,
+    bias_fine_hbm,
+    gain_coarse_hbm,
+    bias_coarse_hbm,
     kernel_fine,
     kernel_coarse,
     out,
     par,
+    acts_fine,
+    acts_coarse,
+    vectors,
     weights_f,
     weights_c,
     sent_f,
@@ -88,8 +91,8 @@
     halo_out_f,
     halo_in_f,
     stats,
-    par_dp,
-    par_rows,
+    par_z,
+    par_xy,
     grad_out,
     grad_in,
     load_sem,
@@ -99,8 +102,7 @@
     recv_frames,
     send_halo,
     recv_halo,
-    send_dp,
-    recv_dp,
+    par_sem,
     send_relay,
     recv_relay,
     ready,
@@ -110,15 +112,20 @@
     width = weights_f.shape[0] // 27
 
     loads = [
-        pltpu.make_async_copy(kernel_coarse, weights_c, load_sem.at[0]),
-        pltpu.make_async_copy(kernel_fine, weights_f, load_sem.at[1]),
+        pltpu.make_async_copy(grad_coarse_hbm, cot.at[:, row], load_sem.at[0]),
+        pltpu.make_async_copy(acts_coarse_hbm, acts_coarse, load_sem.at[1]),
+        pltpu.make_async_copy(acts_fine_hbm, acts_fine, load_sem.at[2]),
+        pltpu.make_async_copy(gain_fine_hbm, vectors.at[0], load_sem.at[3]),
+        pltpu.make_async_copy(bias_fine_hbm, vectors.at[1], load_sem.at[3]),
+        pltpu.make_async_copy(gain_coarse_hbm, vectors.at[2], load_sem.at[3]),
+        pltpu.make_async_copy(bias_coarse_hbm, vectors.at[3], load_sem.at[3]),
+        pltpu.make_async_copy(kernel_coarse, weights_c, load_sem.at[4]),
+        pltpu.make_async_copy(kernel_fine, weights_f, load_sem.at[5]),
     ]
-    for load in loads:
-        load.start()
+    loads[0].start()
 
     even = dp + 1 - 2 * lax.rem(dp, 2)
-    ring = [lax.rem(dp + step, n_dp) for step in (2, n_dp - 2)] if n_dp == 8 else []
-    near_dp = [even] + ring + [lax.rem(even + step, n_dp) for step in (2, n_dp - 2)] if n_dp == 8 else []
+    near_dp = [even] + [lax.rem(core + step, n_dp) for core in (dp, even) for step in (2, n_dp - 2)]
     barrier = pltpu.get_barrier_semaphore()
     for axis, me, count in (("rows", row, n_rows), ("frames", fr, n_frames)):
 
@@ -130,13 +137,10 @@
     for peer in near_dp:
         pl.semaphore_signal(barrier, inc=1, device_id={"dp": peer}, device_id_type=MESH)
 
-    cot[:, row] = grad_coarse[...]
-
-    new, old = iota((LANES, LANES), 0), iota((LANES, LANES), 1)
-    to_new = one_hot(old == fine_position(new))
-    to_old = one_hot(new == fine_position(old))
-    moved = jnp.dot(to_new, acts_fine[...], preferred_element_type=jnp.float32)
-    sent_f[...] = moved.T.astype(jnp.bfloat16)
+    for load in loads[1:]:
+        load.start()
+
+    loads[1].wait()
     place, source = iota((LANES, 32), 0), iota((LANES, 32), 1)
     placed = jnp.dot(one_hot((place & 31) == source), acts_coarse[...], preferred_element_type=jnp.float32)
     quads = placed.T.reshape(n_rows, 4, 8, LANES)
@@ -146,9 +150,19 @@
         folded = jnp.where(quad == k, quads[:, k], folded)
     sent_c[...] = folded.astype(jnp.bfloat16)
 
+    loads[0].wait()
     pl.semaphore_wait(barrier, (n_rows - 1) + (n_frames - 1) + len(near_dp))
-    for peer in ring:
-        pl.semaphore_signal(ready, inc=1, device_id={"dp": peer}, device_id_type=MESH)
+
+    def tell(round_):
+        for peer in near_dp:
+            pl.semaphore_signal(ready.at[round_], inc=1, device_id={"dp": peer}, device_id_type=MESH)
+
+    def told(round_):
+        if near_dp:
+            pl.semaphore_wait(ready.at[round_], len(near_dp))
+
+    def all_of(ref, sem):
+        pltpu.make_async_copy(ref, ref, sem).wait()
 
     def slices(ref, index):
         return ref.at[pl.ds(pl.multiple_of(index * width, width), width)]
@@ -158,15 +172,13 @@
             src, dst = sent_c.at[target], got_c.at[source]
         elif stage == 1:
             src, dst = slices(sent_f, target), got_f.at[source]
-        elif stage == 2:
+        else:
             src, dst = grad_out.at[target], grad_in.at[source]
-        else:
-            src, dst = par_rows.at[row], par_rows.at[source]
         return pltpu.make_async_remote_copy(
             src_ref=src,
             dst_ref=dst,
-            send_sem=send_rows.at[stage, target],
-            recv_sem=recv_rows.at[stage, source],
+            send_sem=send_rows.at[stage],
+            recv_sem=recv_rows.at[stage],
             device_id={"rows": target},
             device_id_type=MESH,
         )
@@ -178,55 +190,44 @@
     def at(y_of, z_of):
         return 4 * y_of + z_of
 
-    def relay(stage, k, slot, target):
+    def relay(stage, kind, slot, target):
         block = (cot.at[:, slot], quart.at[slot])[stage]
         return pltpu.make_async_remote_copy(
             src_ref=block,
             dst_ref=block,
-            send_sem=send_relay.at[stage, k],
-            recv_sem=recv_relay.at[stage, slot],
+            send_sem=send_relay.at[stage],
+            recv_sem=recv_relay.at[stage, kind],
             device_id={"rows": target},
             device_id_type=MESH,
         )
 
     up, down = at(y_up, z), at(y_down, z)
-
-    def routes():
-        own = (None, row, [at(y, z_mate[1]), up, down, at(y, z_mate[2]), at(y, z_mate[3])])
-        return [
-            own,
-            (0, at(y, z_mate[1]), [up, down]),
-            (0, at(y_down, z_mate[0]), [up]),
-            (0, at(y, z_mate[2]), [up, down]),
-            (0, at(y_up, z_mate[1]), [down]),
-            (0, at(y, z_mate[3]), [up, down]),
-            (0, at(y_down, z_mate[2]), [up]),
-            (0, at(y_up, z_mate[3]), [down]),
-            (0, at(y_down, z_mate[1]), []),
-            (0, at(y_down, z_mate[3]), []),
-            (0, at(y_up, z_mate[0]), []),
-            (0, at(y_up, z_mate[2]), []),
-            (0, at(y_far, z_mate[0]), []),
-            (0, at(y_far, z_mate[1]), []),
-            (0, at(y_far, z_mate[2]), []),
-            (0, at(y_far, z_mate[3]), []),
-        ]
+    z_kind, up_kind, down_kind = (None, 0, 2, 4), (1, 7, 5, 7), (7, 3, 7, 6)
 
     def gather_start(stage):
-        for k, target in enumerate(routes()[0][2]):
-            relay(stage, k, row, target).start()
+        relay(stage, z_kind[1], row, at(y, z_mate[1])).start()
+        relay(stage, up_kind[0], row, up).start()
+        relay(stage, down_kind[0], row, down).start()
+        relay(stage, z_kind[2], row, at(y, z_mate[2])).start()
+        relay(stage, z_kind[3], row, at(y, z_mate[3])).start()
+
+    def gather_relay(stage):
+        for kind, y_of, j in ((0, y, 1), (1, y_down, 0), (2, y, 2), (3, y_up, 1), (4, y, 3), (5, y_down, 2), (6, y_up, 3)):
+            slot = at(y_of, z_mate[j])
+            relay(stage, kind, slot, row).wait_recv()
+            if kind in (0, 2, 4):
+                relay(stage, up_kind[j], slot, up).start()
+                relay(stage, down_kind[j], slot, down).start()
+            elif kind in (1, 5):
+                relay(stage, 7, slot, up).start()
+            else:
+                relay(stage, 7, slot, down).start()
 
     def gather_finish(stage):
-        k = 5
-        for _, slot, targets in routes()[1:]:
-            relay(stage, 0, slot, row).wait_recv()
-            for target in targets:
-                relay(stage, k, slot, target).start()
-                k += 1
+        all_of((cot.at[:, pl.ds(0, 8)], quart.at[pl.ds(0, 8)])[stage], recv_relay.at[stage, 7])
 
     def gather_sent(stage):
-        for k in range(15):
-            relay(stage, k, row, up).wait_send()
+        all_of((cot.at[:, pl.ds(0, 15)], quart.at[pl.ds(0, 15)])[stage], send_relay.at[stage])
 
     def rows_send(stage):
         def step(d, carry):
@@ -235,27 +236,21 @@
 
         lax.fori_loop(1, n_rows, step, 0)
 
+    def rows_refs(stage):
+        return (got_c, got_f, grad_in)[stage].at[pl.ds(0, n_rows - 1)]
+
     def rows_wait(stage):
-        def step(d, carry):
-            other = lax.rem(row + n_rows - d, n_rows)
-            rows_copy(stage, other, other).wait_recv()
-            return carry
-
-        lax.fori_loop(1, n_rows, step, 0)
+        all_of(rows_refs(stage), recv_rows.at[stage])
 
     def rows_sent(stage):
-        def step(d, carry):
-            rows_copy(stage, lax.rem(row + d, n_rows), row).wait_send()
-            return carry
-
-        lax.fori_loop(1, n_rows, step, 0)
+        all_of(rows_refs(stage), send_rows.at[stage])
 
     def frames_copy(stage, target, source):
         return pltpu.make_async_remote_copy(
             src_ref=stats.at[stage, fr],
             dst_ref=stats.at[stage, source],
-            send_sem=send_frames.at[stage, target],
-            recv_sem=recv_frames.at[stage, source],
+            send_sem=send_frames.at[stage],
+            recv_sem=recv_frames.at[stage],
             device_id={"frames": target},
             device_id_type=MESH,
         )
@@ -270,12 +265,7 @@
         lax.fori_loop(1, n_frames, step, 0)
 
     def frames_total(stage):
-        def step(d, carry):
-            other = lax.rem(fr + n_frames - d, n_frames)
-            frames_copy(stage, other, other).wait_recv()
-            return carry
-
-        lax.fori_loop(1, n_frames, step, 0)
+        all_of(stats.at[stage, pl.ds(0, n_frames - 1)], recv_frames.at[stage])
         total = stats[stage, 0]
         for k in range(1, n_frames):
             total = total + stats[stage, k]
@@ -310,13 +300,22 @@
     gather_start(0)
     rows_send(0)
     got_c[row] = sent_c[row]
-
-    wide = iota((width, gain_fine.shape[1]), 1) == row * width + iota((width, gain_fine.shape[1]), 0)
+    tell(0)
+
+    loads[2].wait()
+    new, old = iota((LANES, LANES), 0), iota((LANES, LANES), 1)
+    to_new = one_hot(old == fine_position(new))
+    to_old = one_hot(new == fine_position(old))
+    moved = jnp.dot(to_new, acts_fine[...], preferred_element_type=jnp.float32)
+    sent_f[...] = moved.T.astype(jnp.bfloat16)
+    all_of(vectors, load_sem.at[3])
+
+    wide = iota((width, vectors.shape[2]), 1) == row * width + iota((width, vectors.shape[2]), 0)
 
     def column(vector):
-        return row_sum(jnp.where(wide, vector[...], 0.0))
-
-    gain_f, bias_f, gain_c, bias_c = (column(v) for v in (gain_fine, bias_fine, gain_coarse, bias_coarse))
+        return row_sum(jnp.where(wide, vector, 0.0))
+
+    gain_f, bias_f, gain_c, bias_c = (column(vectors[k]) for k in range(4))
     lane, channel = iota((width, LANES), 1), iota((width, LANES), 0)
     chunk = lane >> 4
     diagonal = jnp.where((lane & 31) == channel, lane >> 5, -1)
@@ -369,7 +368,7 @@
             planes.append(after(r[0]) + r[1] + r[2])
         return planes
 
-    gather_finish(0)
+    gather_relay(0)
 
     rows_wait(0)
     pieces = [chunk_swap([got_c[8 * half + j].astype(jnp.float32) for j in range(8)], chunk[:8]) for half in range(2)]
@@ -385,7 +384,10 @@
     rows_send(1)
     got_f[row] = sent_f[pl.ds(pl.multiple_of(row * width, width), width), :]
 
-    loads[0].wait()
+    loads[7].wait()
+    told(0)
+    tell(1)
+    gather_finish(0)
     gathered = cot[...].reshape(2 * n_rows * 16, cot.shape[3])
     nt = (((1,), (1,)), ((), ()))
     prod[...] = lax.dot_general(weights_c[...], gathered, nt, preferred_element_type=jnp.float32)
@@ -415,7 +417,8 @@
 
     halo_wait(0)
     pre_grad_c = (conv_c + halo_in_c[...].astype(jnp.float32)) * slope_c
-    frames_start(1, row_of((row_sum(pre_grad_c), row_sum(pre_grad_c * normed_c)), diagonal))
+    here_c = (row_sum(pre_grad_c), row_sum(pre_grad_c * normed_c))
+    frames_start(1, row_of(here_c, diagonal))
     totals_c = frames_total(1)
     one_c, two_c = column_of(totals_c, diagonal, 0), column_of(totals_c, diagonal, 1)
 
@@ -428,6 +431,7 @@
     quarter = (level_c * 0.25).astype(jnp.bfloat16)
     quart[row] = quarter
     gather_start(1)
+    gather_relay(1)
 
     rows_wait(1)
     swapped = []
@@ -437,7 +441,7 @@
     frames_start(2, row_of((row_sum(values_f), row_sum(values_f * values_f)), diagonal))
     gather_finish(1)
 
-    loads[1].wait()
+    loads[8].wait()
     prod[...] = jnp.dot(
         weights_f[...], quart[...].reshape(n_rows * width, 2 * cells), preferred_element_type=jnp.float32
     )
@@ -451,42 +455,48 @@
     normed_f, slope_f = through(values_f, gain_f, bias_f, mean_f, inv_f)
     halo_wait(1)
     pre_grad_f = (conv_f + halo_in_f[...].astype(jnp.float32)) * slope_f
-    frames_start(3, row_of((row_sum(pre_grad_f), row_sum(pre_grad_f * normed_f)), diagonal))
+    here_f = (row_sum(pre_grad_f), row_sum(pre_grad_f * normed_f))
+    frames_start(3, row_of(here_f, diagonal))
+
+    cells_all = n_dp * 2 * n_frames * cells
+    scale_c, scale_f = 1.0 / cells_all**0.5, 1.0 / (4 * cells_all) ** 0.5
+    n_z, n_xy = 4 * n_dp, 4 * n_frames
+    in_z, in_xy = 4 * dp + z, 4 * fr + y
+
+    def z_copy(target, source):
+        return pltpu.make_async_remote_copy(
+            src_ref=par_z.at[in_z],
+            dst_ref=par_z.at[source],
+            send_sem=par_sem.at[0],
+            recv_sem=par_sem.at[1],
+            device_id={"dp": lax.div(target, 4), "rows": 4 * y + lax.rem(target, 4)},
+            device_id_type=MESH,
+        )
+
+    def xy_copy(target, source):
+        return pltpu.make_async_remote_copy(
+            src_ref=par_xy.at[in_xy],
+            dst_ref=par_xy.at[source],
+            send_sem=par_sem.at[2],
+            recv_sem=par_sem.at[3],
+            device_id={"frames": lax.div(target, 4), "rows": 4 * lax.rem(target, 4) + z},
+            device_id_type=MESH,
+        )
+
+    def each(count, body):
+        def step(d, carry):
+            body(d)
+            return carry
+
+        lax.fori_loop(1, count, step, 0)
+
+    mine = (here_f[1] * scale_f, here_f[0] * scale_f, here_c[1] * scale_c, here_c[0] * scale_c)
+    par_z[in_z] = row_of(mine, diagonal)
+    told(1)
+    each(n_z, lambda d: z_copy(lax.rem(in_z + d, n_z), in_z).start())
+
     totals_f = frames_total(3)
     one_f, two_f = column_of(totals_f, diagonal, 0), column_of(totals_f, diagonal, 1)
-
-    cells_all = n_dp * 2 * n_frames * cells
-    scale_c, scale_f = 1.0 / cells_all**0.5, 1.0 / (4 * cells_all) ** 0.5
-    mine = row_of((two_f * scale_f, one_f * scale_f, two_c * scale_c, one_c * scale_c), diagonal)
-    par_dp[dp] = mine
-
-    def dp_copy(target, source):
-        return pltpu.make_async_remote_copy(
-            src_ref=par_dp.at[dp],
-            dst_ref=par_dp.at[source],
-            send_sem=send_dp.at[target],
-            recv_sem=recv_dp.at[source],
-            device_id={"dp": target},
-            device_id_type=MESH,
-        )
-
-    def dp_start(d, carry):
-        dp_copy(lax.rem(dp + d, n_dp), dp).start()
-        return carry
-
-    def dp_wait(d, carry):
-        other = lax.rem(dp + n_dp - d, n_dp)
-        dp_copy(other, other).wait_recv()
-        return carry
-
-    def dp_sent(d, carry):
-        dp_copy(lax.rem(dp + d, n_dp), dp).wait_send()
-        return carry
-
-    if ring:
-        pl.semaphore_wait(ready, len(ring))
-    if n_dp > 1:
-        lax.fori_loop(1, n_dp, dp_start, 0)
 
     four = [quarter[:, frame * cells : (frame + 1) * cells].astype(jnp.float32) for frame in range(2)]
     cot_f = jnp.concatenate([four[c // 4] for c in range(8)], axis=1)
@@ -498,20 +508,40 @@
     rows_send(2)
     grad_in[row] = grad_out[row]
 
-    if n_dp > 1:
-        lax.fori_loop(1, n_dp, dp_wait, 0)
-    total = par_dp[0]
-    for k in range(1, n_dp):
-        total = total + par_dp[k]
-    par_rows[row] = total
-    rows_send(3)
+    gather_sent(0)
+    gather_sent(1)
+    for stage in range(2):
+        rows_sent(stage)
+    for stage in range(4):
+        all_of(stats.at[stage, pl.ds(0, n_frames - 1)], send_frames.at[stage])
+
+    @pl.when(fr > 0)
+    def _():
+        halo_copy(0).wait_send()
+        halo_copy(1).wait_send()
+
+    all_of(par_z.at[pl.ds(0, n_z - 1)], par_sem.at[1])
+    for k in range(4):
+        total = par_z[k]
+        for j in range(1, n_dp):
+            total = total + par_z[4 * j + k]
+        par_xy[in_xy, k : k + 1] = total
+    each(n_xy, lambda d: xy_copy(lax.rem(in_xy + d, n_xy), in_xy).start())
 
     rows_wait(2)
     back = grad_in[...].reshape(n_rows * width, LANES).astype(jnp.float32).T.astype(jnp.bfloat16)
     out[...] = jnp.dot(to_old, back, preferred_element_type=jnp.float32).astype(out.dtype)
 
-    rows_wait(3)
-    lines = [jnp.concatenate([par_rows[4 * k + j] for k in range(4)], axis=0) for j in range(4)]
+    rows_sent(2)
+    all_of(par_z.at[pl.ds(0, n_z - 1)], par_sem.at[0])
+    all_of(par_xy.at[pl.ds(0, n_xy - 1)], par_sem.at[3])
+    sums = []
+    for k in range(4):
+        total = par_xy[k]
+        for j in range(1, n_frames):
+            total = total + par_xy[4 * j + k]
+        sums.append(total)
+    lines = [jnp.concatenate([sums[k][j : j + 1] for k in range(4)], axis=0) for j in range(4)]
     part = iota(lines[0].shape, 1) >> 5
     for bit in range(2):
         step = 1 << bit
@@ -525,25 +555,13 @@
     for k in range(4):
         par[k] = lines[k]
 
-    gather_sent(0)
-    gather_sent(1)
-    for stage in range(4):
-        rows_sent(stage)
-    for stage in range(4):
-
-        def frames_sent(d, carry, stage=stage):
-            frames_copy(stage, lax.rem(fr + d, n_frames), fr).wait_send()
-            return carry
-
-        lax.fori_loop(1, n_frames, frames_sent, 0)
-
-    @pl.when(fr > 0)
-    def _():
-        halo_copy(0).wait_send()
-        halo_copy(1).wait_send()
-
-    if n_dp > 1:
-        lax.fori_loop(1, n_dp, dp_sent, 0)
+    all_of(par_xy.at[pl.ds(0, n_xy - 1)], par_sem.at[2])
+
+
+def finish(grad, par, out, *vectors):
+    out[...] = grad[...]
+    for k, vector in enumerate(vectors):
+        vector[...] = par[k]
 
 
 def shards(
@@ -567,15 +585,16 @@
     anywhere = pl.BlockSpec(memory_space=pl.ANY)
     dma = pltpu.SemaphoreType.DMA
     taps = kernel_fine.shape[0]
+    held = (pltpu.VMEM((LANES, channels), bf16), pltpu.VMEM((4, channels // LANES, LANES), f32))
     out, par = pl.pallas_call(
         functools.partial(kernel, sizes),
-        out_shape=(
-            jax.ShapeDtypeStruct((LANES, channels), bf16),
-            jax.ShapeDtypeStruct((4, channels // LANES, LANES), f32),
-        ),
-        in_specs=[vmem] * 7 + [anywhere] * 2,
+        out_shape=held,
+        in_specs=[anywhere] * 9,
         out_specs=(vmem, vmem),
         scratch_shapes=[
+            pltpu.VMEM((LANES, channels), bf16),
+            pltpu.VMEM((32, channels), bf16),
+            pltpu.VMEM((4, 1, channels), f32),
             pltpu.VMEM((taps * width, channels), bf16),
             pltpu.VMEM((taps * width, channels), bf16),
             pltpu.VMEM((channels, LANES), bf16),
@@ -590,22 +609,21 @@
             pltpu.VMEM((width, 4 * positions), bf16),
             pltpu.VMEM((width, 4 * positions), bf16),
             pltpu.VMEM((4, n_frames, 1, LANES), f32),
-            pltpu.VMEM((n_dp, 1, LANES), f32),
-            pltpu.VMEM((n_rows, 1, LANES), f32),
+            pltpu.VMEM((4 * n_dp, 1, LANES), f32),
+            pltpu.VMEM((4 * n_frames, 4, LANES), f32),
             pltpu.VMEM((n_rows, width, LANES), bf16),
             pltpu.VMEM((n_rows, width, LANES), bf16),
-            dma((2,)),
-            dma((4, n_rows)),
-            dma((4, n_rows)),
-            dma((4, n_frames)),
-            dma((4, n_frames)),
+            dma((6,)),
+            dma((3,)),
+            dma((3,)),
+            dma((4,)),
+            dma((4,)),
             dma((2,)),
             dma((2,)),
-            dma((n_dp,)),
-            dma((n_dp,)),
-            dma((2, 15)),
-            dma((2, n_rows)),
-            pltpu.SemaphoreType.REGULAR,
+            dma((4,)),
+            dma((2,)),
+            dma((2, 8)),
+            pltpu.SemaphoreType.REGULAR((2,)),
         ],
         compiler_params=pltpu.CompilerParams(collective_id=0, has_side_effects=True),
         name="levels",
@@ -620,8 +638,15 @@
         kernel_fine.reshape(taps * width, channels),
         kernel_coarse.reshape(taps * width, channels),
     )
-    vectors = par.reshape(4, channels)
-    return (out.reshape(acts_fine.shape), vectors[0], vectors[1], vectors[2], vectors[3])
+    vector = jax.ShapeDtypeStruct((channels // LANES, LANES), f32)
+    grad, *vectors = pl.pallas_call(
+        finish,
+        out_shape=(jax.ShapeDtypeStruct((LANES, channels), bf16), vector, vector, vector, vector),
+        in_specs=[vmem, vmem],
+        out_specs=(vmem,) * 5,
+        name="finish",
+    )(*(pltpu.with_memory_space_constraint(x, pltpu.VMEM) for x in (out, par)))
+    return (grad.reshape(acts_fine.shape), *(v.reshape(channels) for v in vectors))
 
 
 def solution(mesh):

time: 78.9 us -> 68.8 us (0.87)
  Pallas kernels: 75.3 us -> 68 us
  local copies, waits for them, and re-layouts: 2.85 us -> 0 us
    pallas_call x1 -> x2, Pallas kernels: 75.3 us -> 68 us  [the longest x1 67.4 us: shards(): pl.pallas_call(functools.partial(kernel, sizes), out_shape=held, in_specs...]
    unnamed x1 -> x0, local copies, waits for them, and re-layouts: 1.57 us -> none
    squeeze x1 -> x0, local copies, waits for them, and re-layouts: 1.29 us -> none  [shards(): vectors[3]]
where the time goes in v2:
time: 68.8 us; the launch traced here: 68.7 us
  Pallas kernels  68 us (99%)
    pallas_call x1, Pallas kernels, shards(): pl.pallas_call(functools.partial(kernel, sizes), out_shape=held, in_specs...  67.4 us

profile of v2, /device:TPU:1, one launch (start us, length us, event | category | flops | bytes accessed | tf_op | source)
XLA Modules:
  0.0 68.7 jit_solution(6875566365173770056)
XLA Ops:
  0.6 67.4 %levels.1 = (bf16[128,512]{1,0:T(8,128)(2,1)S(1)}, f32[4,4,128]{2,1,0:T(4,128)S(1)}) custom-call(bf16[128,512]{1,0:T(8,128)(2,1)} %bitcast.16, bf16[32,512]{1,0:T(8,128)(2,1)} %bitcast.17, bf16[2,16,512]{2,1,0:T(8,128)(2,1)} %bitcast.18, f32[1,512]{1,0:T(1,128)} %bitcast.19, f32[1,512]{1,0:T(1,128)} %bitcast.20, f32[1,512]{1,0:T(1,128)} %bitcast.21, ...), custom_call_target="tpu_custom_call" | custom-call | tf_op jit(solution)/shard_map/levels/pallas_call | solution.py:589
  68.0 0.7 finish.1

commit v3 on v2

--- a/solution.py
+++ b/solution.py
@@ -90,6 +90,10 @@
     halo_in_c,
     halo_out_f,
     halo_in_f,
+    here_vals_c,
+    prev_vals_c,
+    here_vals_f,
+    prev_vals_f,
     stats,
     par_z,
     par_xy,
@@ -102,6 +106,7 @@
     recv_frames,
     send_halo,
     recv_halo,
+    pass_sem,
     par_sem,
     send_relay,
     recv_relay,
@@ -212,7 +217,7 @@
         relay(stage, z_kind[3], row, at(y, z_mate[3])).start()
 
     def gather_relay(stage):
-        for kind, y_of, j in ((0, y, 1), (1, y_down, 0), (2, y, 2), (3, y_up, 1), (4, y, 3), (5, y_down, 2), (6, y_up, 3)):
+        for kind, y_of, j in ((0, y, 1), (1, y_down, 0), (2, y, 2), (4, y, 3), (3, y_up, 1), (5, y_down, 2), (6, y_up, 3)):
             slot = at(y_of, z_mate[j])
             relay(stage, kind, slot, row).wait_recv()
             if kind in (0, 2, 4):
@@ -309,6 +314,32 @@
     moved = jnp.dot(to_new, acts_fine[...], preferred_element_type=jnp.float32)
     sent_f[...] = moved.T.astype(jnp.bfloat16)
     all_of(vectors, load_sem.at[3])
+
+    def pass_on(stage):
+        here, there = ((here_vals_c, prev_vals_c), (here_vals_f, prev_vals_f))[stage]
+        return pltpu.make_async_remote_copy(
+            src_ref=here,
+            dst_ref=there,
+            send_sem=pass_sem.at[0, stage],
+            recv_sem=pass_sem.at[1, stage],
+            device_id={"frames": lax.rem(fr + 1, n_frames)},
+            device_id_type=MESH,
+        )
+
+    def pass_send(stage):
+        @pl.when(fr < n_frames - 1)
+        def _():
+            pass_on(stage).start()
+
+    def pass_wait(stage):
+        @pl.when(fr > 0)
+        def _():
+            pass_on(stage).wait_recv()
+
+        @pl.when(fr == 0)
+        def _():
+            into = (prev_vals_c, prev_vals_f)[stage]
+            into[...] = jnp.zeros_like(into)
 
     wide = iota((width, vectors.shape[2]), 1) == row * width + iota((width, vectors.shape[2]), 0)
 
@@ -380,6 +411,8 @@
         ],
         axis=1,
     )
+    here_vals_c[...] = values_c.astype(jnp.bfloat16)
+    pass_send(0)
     frames_start(0, row_of((row_sum(values_c), row_sum(values_c * values_c)), diagonal))
     rows_send(1)
     got_f[row] = sent_f[pl.ds(pl.multiple_of(row * width, width), width), :]
@@ -391,8 +424,8 @@
     gathered = cot[...].reshape(2 * n_rows * 16, cot.shape[3])
     nt = (((1,), (1,)), ((), ()))
     prod[...] = lax.dot_general(weights_c[...], gathered, nt, preferred_element_type=jnp.float32)
-    halo_out_c[:, 0:cells] = coarse_frame(0).astype(halo_out_c.dtype)
-    halo_out_c[:, cells:] = coarse_frame(1).astype(halo_out_c.dtype)
+    conv_before = jnp.concatenate([coarse_frame(0), coarse_frame(1)], axis=1)
+    halo_out_c[...] = conv_before.astype(halo_out_c.dtype)
     halo_send(0)
     conv_c = jnp.concatenate([coarse_frame(2), coarse_frame(3)], axis=1)
     picked = one_hot(wide)
@@ -415,10 +448,27 @@
     mean_c, inv_c = norm_of(frames_total(0), entries_c)
     normed_c, slope_c = through(values_c, gain_c, bias_c, mean_c, inv_c)
 
+    def sums_of(conv, normed, slope, conv_before, normed_before, slope_before):
+        now, then = conv * slope, conv_before * slope_before
+        pairs = ((row_sum(now), row_sum(then)), (row_sum(now * normed), row_sum(then * normed_before)))
+        return tuple(own + jnp.where(fr > 0, earlier, 0.0) for own, earlier in pairs)
+
+    pass_wait(0)
+    before_c = through(prev_vals_c[...].astype(jnp.float32), gain_c, bias_c, mean_c, inv_c)
+    here_c = sums_of(conv_c, normed_c, slope_c, conv_before, *before_c)
+    frames_start(1, row_of(here_c, diagonal))
+
+    rows_wait(1)
+    swapped = []
+    for half in range(2):
+        swapped.append(chunk_swap([got_f[8 * half + j].astype(jnp.float32) for j in range(8)], chunk))
+    values_f = jnp.concatenate([swapped[half][c] for c in range(8) for half in range(2)], axis=1)
+    here_vals_f[...] = values_f.astype(jnp.bfloat16)
+    pass_send(1)
+    frames_start(2, row_of((row_sum(values_f), row_sum(values_f * values_f)), diagonal))
+
     halo_wait(0)
     pre_grad_c = (conv_c + halo_in_c[...].astype(jnp.float32)) * slope_c
-    here_c = (row_sum(pre_grad_c), row_sum(pre_grad_c * normed_c))
-    frames_start(1, row_of(here_c, diagonal))
     totals_c = frames_total(1)
     one_c, two_c = column_of(totals_c, diagonal, 0), column_of(totals_c, diagonal, 1)
 
@@ -432,31 +482,21 @@
     quart[row] = quarter
     gather_start(1)
     gather_relay(1)
-
-    rows_wait(1)
-    swapped = []
-    for half in range(2):
-        swapped.append(chunk_swap([got_f[8 * half + j].astype(jnp.float32) for j in range(8)], chunk))
-    values_f = jnp.concatenate([swapped[half][c] for c in range(8) for half in range(2)], axis=1)
-    frames_start(2, row_of((row_sum(values_f), row_sum(values_f * values_f)), diagonal))
+    mean_f, inv_f = norm_of(frames_total(2), entries_f)
+    normed_f, slope_f = through(here_vals_f[...].astype(jnp.float32), gain_f, bias_f, mean_f, inv_f)
+    pass_wait(1)
+    before_f = through(prev_vals_f[...].astype(jnp.float32), gain_f, bias_f, mean_f, inv_f)
     gather_finish(1)
 
     loads[8].wait()
     prod[...] = jnp.dot(
         weights_f[...], quart[...].reshape(n_rows * width, 2 * cells), preferred_element_type=jnp.float32
     )
-    for which in range(2):
-        halo_out_f[:, which * 4 * cells : (which + 1) * 4 * cells] = jnp.concatenate(
-            fine_frame(which), axis=1
-        ).astype(halo_out_f.dtype)
+    conv_before = jnp.concatenate(fine_frame(0) + fine_frame(1), axis=1)
+    halo_out_f[...] = conv_before.astype(halo_out_f.dtype)
     halo_send(1)
     conv_f = jnp.concatenate(fine_frame(2) + fine_frame(3), axis=1)
-    mean_f, inv_f = norm_of(frames_total(2), entries_f)
-    normed_f, slope_f = through(values_f, gain_f, bias_f, mean_f, inv_f)
-    halo_wait(1)
-    pre_grad_f = (conv_f + halo_in_f[...].astype(jnp.float32)) * slope_f
-    here_f = (row_sum(pre_grad_f), row_sum(pre_grad_f * normed_f))
-    frames_start(3, row_of(here_f, diagonal))
+    here_f = sums_of(conv_f, normed_f, slope_f, conv_before, *before_f)
 
     cells_all = n_dp * 2 * n_frames * cells
     scale_c, scale_f = 1.0 / cells_all**0.5, 1.0 / (4 * cells_all) ** 0.5
@@ -495,6 +535,9 @@
     told(1)
     each(n_z, lambda d: z_copy(lax.rem(in_z + d, n_z), in_z).start())
 
+    frames_start(3, row_of(here_f, diagonal))
+    halo_wait(1)
+    pre_grad_f = (conv_f + halo_in_f[...].astype(jnp.float32)) * slope_f
     totals_f = frames_total(3)
     one_f, two_f = column_of(totals_f, diagonal, 0), column_of(totals_f, diagonal, 1)
 
@@ -519,6 +562,11 @@
     def _():
         halo_copy(0).wait_send()
         halo_copy(1).wait_send()
+
+    @pl.when(fr < n_frames - 1)
+    def _():
+        pass_on(0).wait_send()
+        pass_on(1).wait_send()
 
     all_of(par_z.at[pl.ds(0, n_z - 1)], par_sem.at[1])
     for k in range(4):
@@ -608,6 +656,10 @@
             pltpu.VMEM((width, positions), bf16),
             pltpu.VMEM((width, 4 * positions), bf16),
             pltpu.VMEM((width, 4 * positions), bf16),
+            pltpu.VMEM((width, positions), bf16),
+            pltpu.VMEM((width, positions), bf16),
+            pltpu.VMEM((width, 4 * positions), bf16),
+            pltpu.VMEM((width, 4 * positions), bf16),
             pltpu.VMEM((4, n_frames, 1, LANES), f32),
             pltpu.VMEM((4 * n_dp, 1, LANES), f32),
             pltpu.VMEM((4 * n_frames, 4, LANES), f32),
@@ -620,6 +672,7 @@
             dma((4,)),
             dma((2,)),
             dma((2,)),
+            dma((2, 2)),
             dma((4,)),
             dma((2,)),
             dma((2, 8)),

time: 68.8 us -> 57.3 us (0.83)
  Pallas kernels: 68 us -> 56.6 us
    pallas_call x1, Pallas kernels: 67.4 us -> 55.9 us  [shards(): pl.pallas_call(functools.partial(kernel, sizes), out_shape=held, in_specs...]
where the time goes in v3:
time: 57.3 us; the launch traced here: 57.2 us
  Pallas kernels  56.6 us (99%)
  between operations  0.64 us (1%)
    pallas_call x1, Pallas kernels, shards(): pl.pallas_call(functools.partial(kernel, sizes), out_shape=held, in_specs...  55.9 us

profile of v3, /device:TPU:1, one launch (start us, length us, event | category | flops | bytes accessed | tf_op | source)
XLA Modules:
  0.0 57.2 jit_solution(17772117105798033837)
XLA Ops:
  0.6 55.9 %levels.1 = (bf16[128,512]{1,0:T(8,128)(2,1)S(1)}, f32[4,4,128]{2,1,0:T(4,128)S(1)}) custom-call(bf16[128,512]{1,0:T(8,128)(2,1)} %bitcast.16, bf16[32,512]{1,0:T(8,128)(2,1)} %bitcast.17, bf16[2,16,512]{2,1,0:T(8,128)(2,1)} %bitcast.18, f32[1,512]{1,0:T(1,128)} %bitcast.19, f32[1,512]{1,0:T(1,128)} %bitcast.20, f32[1,512]{1,0:T(1,128)} %bitcast.21, ...), custom_call_target="tpu_custom_call" | custom-call | tf_op jit(solution)/shard_map/levels/pallas_call | solution.py:637
  56.5 0.7 %finish.1 = (bf16[128,512]{1,0:T(8,128)(2,1)}, f32[4,128]{1,0:T(4,128)}, f32[4,128]{1,0:T(4,128)}, f32[4,128]{1,0:T(4,128)}, f32[4,128]{1,0:T(4,128)}) custom-call(bf16[128,512]{1,0:T(8,128)(2,1)S(1)} %get-tuple-element.12.grad, f32[4,4,128]{2,1,0:T(4,128)S(1)} %get-tuple-element.13.par), custom_call_target="tpu_custom_call" | custom-call | tf_op jit(solution)/shard_map/finish/pallas_call | solution.py:695

commit v4 on v3

--- a/solution.py
+++ b/solution.py
@@ -206,30 +206,22 @@
             device_id_type=MESH,
         )
 
-    up, down = at(y_up, z), at(y_down, z)
-    z_kind, up_kind, down_kind = (None, 0, 2, 4), (1, 7, 5, 7), (7, 3, 7, 6)
+    up, down, far = at(y_up, z), at(y_down, z), at(y_far, z)
+    last = 3
 
     def gather_start(stage):
-        relay(stage, z_kind[1], row, at(y, z_mate[1])).start()
-        relay(stage, up_kind[0], row, up).start()
-        relay(stage, down_kind[0], row, down).start()
-        relay(stage, z_kind[2], row, at(y, z_mate[2])).start()
-        relay(stage, z_kind[3], row, at(y, z_mate[3])).start()
+        for kind, target in ((0, at(y, z_mate[1])), (last, up), (last, down), (1, at(y, z_mate[2])), (2, at(y, z_mate[3])), (last, far)):
+            relay(stage, kind, row, target).start()
 
     def gather_relay(stage):
-        for kind, y_of, j in ((0, y, 1), (1, y_down, 0), (2, y, 2), (4, y, 3), (3, y_up, 1), (5, y_down, 2), (6, y_up, 3)):
-            slot = at(y_of, z_mate[j])
-            relay(stage, kind, slot, row).wait_recv()
-            if kind in (0, 2, 4):
-                relay(stage, up_kind[j], slot, up).start()
-                relay(stage, down_kind[j], slot, down).start()
-            elif kind in (1, 5):
-                relay(stage, 7, slot, up).start()
-            else:
-                relay(stage, 7, slot, down).start()
+        for j in (1, 2, 3):
+            slot = at(y, z_mate[j])
+            relay(stage, j - 1, slot, row).wait_recv()
+            for target in (far, up, down):
+                relay(stage, last, slot, target).start()
 
     def gather_finish(stage):
-        all_of((cot.at[:, pl.ds(0, 8)], quart.at[pl.ds(0, 8)])[stage], recv_relay.at[stage, 7])
+        all_of((cot.at[:, pl.ds(0, 12)], quart.at[pl.ds(0, 12)])[stage], recv_relay.at[stage, last])
 
     def gather_sent(stage):
         all_of((cot.at[:, pl.ds(0, 15)], quart.at[pl.ds(0, 15)])[stage], send_relay.at[stage])
@@ -533,7 +525,7 @@
     mine = (here_f[1] * scale_f, here_f[0] * scale_f, here_c[1] * scale_c, here_c[0] * scale_c)
     par_z[in_z] = row_of(mine, diagonal)
     told(1)
-    each(n_z, lambda d: z_copy(lax.rem(in_z + d, n_z), in_z).start())
+    each(n_z, lambda d: z_copy(lax.rem(in_z + 1 + lax.rem(d + n_z // 2 - 2, n_z - 1), n_z), in_z).start())
 
     frames_start(3, row_of(here_f, diagonal))
     halo_wait(1)
@@ -675,7 +667,7 @@
             dma((2, 2)),
             dma((4,)),
             dma((2,)),
-            dma((2, 8)),
+            dma((2, 4)),
             pltpu.SemaphoreType.REGULAR((2,)),
         ],
         compiler_params=pltpu.CompilerParams(collective_id=0, has_side_effects=True),

time: 57.3 us -> 52.6 us (0.918)
  Pallas kernels: 56.6 us -> 51.8 us
    pallas_call x1, Pallas kernels: 55.9 us -> 51.2 us  [shards(): pl.pallas_call(functools.partial(kernel, sizes), out_shape=held, in_specs...]
where the time goes in v4:
time: 52.6 us; the launch traced here: 52.5 us
  Pallas kernels  51.8 us (98%)
  between operations  0.64 us (1%)
    pallas_call x1, Pallas kernels, shards(): pl.pallas_call(functools.partial(kernel, sizes), out_shape=held, in_specs...  51.2 us

profile of v4, /device:TPU:1, one launch (start us, length us, event | category | flops | bytes accessed | tf_op | source)
XLA Modules:
  0.0 52.5 jit_solution(10827623163036213916)
XLA Ops:
  0.6 51.2 %levels.1 = (bf16[128,512]{1,0:T(8,128)(2,1)S(1)}, f32[4,4,128]{2,1,0:T(4,128)S(1)}) custom-call(bf16[128,512]{1,0:T(8,128)(2,1)} %bitcast.16, bf16[32,512]{1,0:T(8,128)(2,1)} %bitcast.17, bf16[2,16,512]{2,1,0:T(8,128)(2,1)} %bitcast.18, f32[1,512]{1,0:T(1,128)} %bitcast.19, f32[1,512]{1,0:T(1,128)} %bitcast.20, f32[1,512]{1,0:T(1,128)} %bitcast.21, ...), custom_call_target="tpu_custom_call" | custom-call | tf_op jit(solution)/shard_map/levels/pallas_call | solution.py:629
  51.8 0.7 %finish.1 = (bf16[128,512]{1,0:T(8,128)(2,1)}, f32[4,128]{1,0:T(4,128)}, f32[4,128]{1,0:T(4,128)}, f32[4,128]{1,0:T(4,128)}, f32[4,128]{1,0:T(4,128)}) custom-call(bf16[128,512]{1,0:T(8,128)(2,1)S(1)} %get-tuple-element.12.grad, f32[4,4,128]{2,1,0:T(4,128)S(1)} %get-tuple-element.13.par), custom_call_target="tpu_custom_call" | custom-call | tf_op jit(solution)/shard_map/finish/pallas_call | solution.py:687

commit v5 on v4

--- a/solution.py
+++ b/solution.py
@@ -85,7 +85,9 @@
     got_c,
     cot,
     quart,
-    prod,
+    prod_0,
+    prod_1,
+    prod_2,
     halo_out_c,
     halo_in_c,
     halo_out_f,
@@ -113,6 +115,7 @@
     ready,
 ):
     n_dp, n_frames, n_rows = sizes
+    prods = (prod_0, prod_1, prod_2)
     dp, fr, row = lax.axis_index("dp"), lax.axis_index("frames"), lax.axis_index("rows")
     width = weights_f.shape[0] // 27
 
@@ -131,16 +134,16 @@
 
     even = dp + 1 - 2 * lax.rem(dp, 2)
     near_dp = [even] + [lax.rem(core + step, n_dp) for core in (dp, even) for step in (2, n_dp - 2)]
+    y, z = lax.div(row, 4), lax.rem(row, 4)
+    z_mate = (z, z + 1 - 2 * lax.rem(z, 2), lax.rem(z + 2, 4), 3 - z)
+    y_up, y_down, y_far = lax.rem(y + 1, 4), lax.rem(y + 3, 4), lax.rem(y + 2, 4)
+    greeted = [{"rows": 4 * y_far + z_of} for z_of in z_mate] + [{"dp": peer} for peer in near_dp]
+    greeted += [{"rows": 4 * y_of + z_of} for y_of in (y_up, y_down) for z_of in z_mate]
+    greeted += [{"rows": 4 * y + z_of} for z_of in z_mate[1:]]
+    greeted += [{"frames": lax.rem(fr + step, n_frames)} for step in range(1, n_frames)]
     barrier = pltpu.get_barrier_semaphore()
-    for axis, me, count in (("rows", row, n_rows), ("frames", fr, n_frames)):
-
-        def greet(d, carry, axis=axis, me=me, count=count):
-            pl.semaphore_signal(barrier, inc=1, device_id={axis: lax.rem(me + d, count)}, device_id_type=MESH)
-            return carry
-
-        lax.fori_loop(1, count, greet, 0)
-    for peer in near_dp:
-        pl.semaphore_signal(barrier, inc=1, device_id={"dp": peer}, device_id_type=MESH)
+    for peer in greeted:
+        pl.semaphore_signal(barrier, inc=1, device_id=peer, device_id_type=MESH)
 
     for load in loads[1:]:
         load.start()
@@ -156,7 +159,7 @@
     sent_c[...] = folded.astype(jnp.bfloat16)
 
     loads[0].wait()
-    pl.semaphore_wait(barrier, (n_rows - 1) + (n_frames - 1) + len(near_dp))
+    pl.semaphore_wait(barrier, len(greeted))
 
     def tell(round_):
         for peer in near_dp:
@@ -188,10 +191,6 @@
             device_id_type=MESH,
         )
 
-    y, z = lax.div(row, 4), lax.rem(row, 4)
-    z_mate = (z, z + 1 - 2 * lax.rem(z, 2), lax.rem(z + 2, 4), 3 - z)
-    y_up, y_down, y_far = lax.rem(y + 1, 4), lax.rem(y + 3, 4), lax.rem(y + 2, 4)
-
     def at(y_of, z_of):
         return 4 * y_of + z_of
 
@@ -361,8 +360,7 @@
         return jnp.where(right, pltpu.roll(x, cells - 1, 1), 0.0)
 
     def product(depth, tap, frame):
-        at = (depth * 9 + tap) * width
-        return prod[at : at + width, frame * cells : (frame + 1) * cells]
+        return prods[depth][tap * width : (tap + 1) * width, frame * cells : (frame + 1) * cells]
 
     def spatial_taps(which):
         terms = (((0, 0),), ((1, 0), (0, 1)), ((2, 0), (1, 1)), ((2, 1),))[which]
@@ -404,8 +402,8 @@
         axis=1,
     )
     here_vals_c[...] = values_c.astype(jnp.bfloat16)
+    frames_start(0, row_of((row_sum(values_c), row_sum(values_c * values_c)), diagonal))
     pass_send(0)
-    frames_start(0, row_of((row_sum(values_c), row_sum(values_c * values_c)), diagonal))
     rows_send(1)
     got_f[row] = sent_f[pl.ds(pl.multiple_of(row * width, width), width), :]
 
@@ -415,10 +413,20 @@
     gather_finish(0)
     gathered = cot[...].reshape(2 * n_rows * 16, cot.shape[3])
     nt = (((1,), (1,)), ((), ()))
-    prod[...] = lax.dot_general(weights_c[...], gathered, nt, preferred_element_type=jnp.float32)
-    conv_before = jnp.concatenate([coarse_frame(0), coarse_frame(1)], axis=1)
+
+    def depth_c(depth):
+        at = depth * 9 * width
+        prods[depth][...] = lax.dot_general(
+            weights_c[at : at + 9 * width, :], gathered, nt, preferred_element_type=jnp.float32
+        )
+
+    depth_c(0)
+    first = coarse_frame(0)
+    depth_c(1)
+    second = coarse_frame(1)
+    conv_before = jnp.concatenate([first, second], axis=1)
     halo_out_c[...] = conv_before.astype(halo_out_c.dtype)
-    halo_send(0)
+    depth_c(2)
     conv_c = jnp.concatenate([coarse_frame(2), coarse_frame(3)], axis=1)
     picked = one_hot(wide)
     cot_c = lax.dot_general(picked, gathered, nt, preferred_element_type=jnp.float32)
@@ -449,6 +457,7 @@
     before_c = through(prev_vals_c[...].astype(jnp.float32), gain_c, bias_c, mean_c, inv_c)
     here_c = sums_of(conv_c, normed_c, slope_c, conv_before, *before_c)
     frames_start(1, row_of(here_c, diagonal))
+    halo_send(0)
 
     rows_wait(1)
     swapped = []
@@ -456,20 +465,21 @@
         swapped.append(chunk_swap([got_f[8 * half + j].astype(jnp.float32) for j in range(8)], chunk))
     values_f = jnp.concatenate([swapped[half][c] for c in range(8) for half in range(2)], axis=1)
     here_vals_f[...] = values_f.astype(jnp.bfloat16)
+    frames_start(2, row_of((row_sum(values_f), row_sum(values_f * values_f)), diagonal))
     pass_send(1)
-    frames_start(2, row_of((row_sum(values_f), row_sum(values_f * values_f)), diagonal))
 
     halo_wait(0)
     pre_grad_c = (conv_c + halo_in_c[...].astype(jnp.float32)) * slope_c
+    base_c, lean_c = cot_c + inv_c * (gain_c * pre_grad_c), inv_c * normed_c
     totals_c = frames_total(1)
     one_c, two_c = column_of(totals_c, diagonal, 0), column_of(totals_c, diagonal, 1)
 
-    def level(cot, normed, pre_grad, gain, inv, one, two, entries):
+    def level(base, slope, gain, inv, one, two, entries):
         group_one = group_total(gain * one) / entries
         group_two = group_total(gain * two) / entries
-        return cot + inv * (gain * pre_grad - group_one - normed * group_two)
-
-    level_c = level(cot_c, normed_c, pre_grad_c, gain_c, inv_c, one_c, two_c, entries_c)
+        return base - inv * group_one - slope * group_two
+
+    level_c = level(base_c, lean_c, gain_c, inv_c, one_c, two_c, entries_c)
     quarter = (level_c * 0.25).astype(jnp.bfloat16)
     quart[row] = quarter
     gather_start(1)
@@ -481,12 +491,22 @@
     gather_finish(1)
 
     loads[8].wait()
-    prod[...] = jnp.dot(
-        weights_f[...], quart[...].reshape(n_rows * width, 2 * cells), preferred_element_type=jnp.float32
-    )
-    conv_before = jnp.concatenate(fine_frame(0) + fine_frame(1), axis=1)
+    quarters = quart[...].reshape(n_rows * width, 2 * cells)
+
+    def depth_f(depth):
+        at = depth * 9 * width
+        prods[depth][...] = jnp.dot(
+            weights_f[at : at + 9 * width, :], quarters, preferred_element_type=jnp.float32
+        )
+
+    depth_f(0)
+    first = fine_frame(0)
+    depth_f(1)
+    second = fine_frame(1)
+    conv_before = jnp.concatenate(first + second, axis=1)
     halo_out_f[...] = conv_before.astype(halo_out_f.dtype)
     halo_send(1)
+    depth_f(2)
     conv_f = jnp.concatenate(fine_frame(2) + fine_frame(3), axis=1)
     here_f = sums_of(conv_f, normed_f, slope_f, conv_before, *before_f)
 
@@ -495,47 +515,45 @@
     n_z, n_xy = 4 * n_dp, 4 * n_frames
     in_z, in_xy = 4 * dp + z, 4 * fr + y
 
-    def z_copy(target, source):
+    def z_copy(dp_of, z_of):
         return pltpu.make_async_remote_copy(
             src_ref=par_z.at[in_z],
-            dst_ref=par_z.at[source],
+            dst_ref=par_z.at[in_z],
             send_sem=par_sem.at[0],
             recv_sem=par_sem.at[1],
-            device_id={"dp": lax.div(target, 4), "rows": 4 * y + lax.rem(target, 4)},
+            device_id={"dp": dp_of, "rows": 4 * y + z_of},
             device_id_type=MESH,
         )
 
-    def xy_copy(target, source):
+    def xy_copy(fr_of, y_of):
         return pltpu.make_async_remote_copy(
             src_ref=par_xy.at[in_xy],
-            dst_ref=par_xy.at[source],
+            dst_ref=par_xy.at[in_xy],
             send_sem=par_sem.at[2],
             recv_sem=par_sem.at[3],
-            device_id={"frames": lax.div(target, 4), "rows": 4 * lax.rem(target, 4) + z},
+            device_id={"frames": fr_of, "rows": 4 * y_of + z},
             device_id_type=MESH,
         )
-
-    def each(count, body):
-        def step(d, carry):
-            body(d)
-            return carry
-
-        lax.fori_loop(1, count, step, 0)
 
     mine = (here_f[1] * scale_f, here_f[0] * scale_f, here_c[1] * scale_c, here_c[0] * scale_c)
     par_z[in_z] = row_of(mine, diagonal)
     told(1)
-    each(n_z, lambda d: z_copy(lax.rem(in_z + 1 + lax.rem(d + n_z // 2 - 2, n_z - 1), n_z), in_z).start())
-
+    for step in (4, 5, 3, 6, 2, 7, 1):
+        there = lax.rem(dp + step, n_dp)
+        for k in range(4):
+            z_copy(there, k).start()
+    for k in (1, 2, 3):
+        z_copy(dp, z_mate[k]).start()
     frames_start(3, row_of(here_f, diagonal))
     halo_wait(1)
     pre_grad_f = (conv_f + halo_in_f[...].astype(jnp.float32)) * slope_f
+    four = [quarter[:, frame * cells : (frame + 1) * cells].astype(jnp.float32) for frame in range(2)]
+    cot_f = jnp.concatenate([four[c // 4] for c in range(8)], axis=1)
+    base_f, lean_f = cot_f + inv_f * (gain_f * pre_grad_f), inv_f * normed_f
     totals_f = frames_total(3)
     one_f, two_f = column_of(totals_f, diagonal, 0), column_of(totals_f, diagonal, 1)
 
-    four = [quarter[:, frame * cells : (frame + 1) * cells].astype(jnp.float32) for frame in range(2)]
-    cot_f = jnp.concatenate([four[c // 4] for c in range(8)], axis=1)
-    level_f = level(cot_f, normed_f, pre_grad_f, gain_f, inv_f, one_f, two_f, entries_f)
+    level_f = level(base_f, lean_f, gain_f, inv_f, one_f, two_f, entries_f)
     for half in range(2):
         planes = [level_f[:, c * cells + half * LANES : c * cells + (half + 1) * LANES] for c in range(8)]
         for j, block in enumerate(chunk_swap(planes, chunk)):
@@ -566,7 +584,12 @@
         for j in range(1, n_dp):
             total = total + par_z[4 * j + k]
         par_xy[in_xy, k : k + 1] = total
-    each(n_xy, lambda d: xy_copy(lax.rem(in_xy + d, n_xy), in_xy).start())
+    for step in (2, 1, 3):
+        there = lax.rem(fr + step, n_frames)
+        for k in range(4):
+            xy_copy(there, k).start()
+    for k in (y_far, y_up, y_down):
+        xy_copy(fr, k).start()
 
     rows_wait(2)
     back = grad_in[...].reshape(n_rows * width, LANES).astype(jnp.float32).T.astype(jnp.bfloat16)
@@ -643,7 +666,9 @@
             pltpu.VMEM((n_rows, 8, LANES), bf16),
             pltpu.VMEM((2, n_rows, 16, channels), bf16),
             pltpu.VMEM((n_rows, width, positions), bf16),
-            pltpu.VMEM((taps * width, positions), f32),
+            pltpu.VMEM((9 * width, positions), f32),
+            pltpu.VMEM((9 * width, positions), f32),
+            pltpu.VMEM((9 * width, positions), f32),
             pltpu.VMEM((width, positions), bf16),
             pltpu.VMEM((width, positions), bf16),
             pltpu.VMEM((width, 4 * positions), bf16),

time: 52.6 us -> 51.6 us (0.981)
  Pallas kernels: 51.8 us -> 50.8 us
    pallas_call x1, Pallas kernels: 51.2 us -> 50.1 us  [shards(): pl.pallas_call(functools.partial(kernel, sizes), out_shape=held, in_specs...]
where the time goes in v5:
time: 51.6 us; the launch traced here: 51.5 us
  Pallas kernels  50.8 us (98%)
  between operations  0.64 us (1%)
    pallas_call x1, Pallas kernels, shards(): pl.pallas_call(functools.partial(kernel, sizes), out_shape=held, in_specs...  50.1 us

profile of v5, /device:TPU:1, one launch (start us, length us, event | category | flops | bytes accessed | tf_op | source)
XLA Modules:
  0.0 51.5 jit_solution(2180068722048591283)
XLA Ops:
  0.6 50.1 %levels.1 = (bf16[128,512]{1,0:T(8,128)(2,1)S(1)}, f32[4,4,128]{2,1,0:T(4,128)S(1)}) custom-call(bf16[128,512]{1,0:T(8,128)(2,1)} %bitcast.16, bf16[32,512]{1,0:T(8,128)(2,1)} %bitcast.17, bf16[2,16,512]{2,1,0:T(8,128)(2,1)} %bitcast.18, f32[1,512]{1,0:T(1,128)} %bitcast.19, f32[1,512]{1,0:T(1,128)} %bitcast.20, f32[1,512]{1,0:T(1,128)} %bitcast.21, ...), custom_call_target="tpu_custom_call" | custom-call | tf_op jit(solution)/shard_map/levels/pallas_call | solution.py:652
  50.8 0.7 %finish.1 = (bf16[128,512]{1,0:T(8,128)(2,1)}, f32[4,128]{1,0:T(4,128)}, f32[4,128]{1,0:T(4,128)}, f32[4,128]{1,0:T(4,128)}, f32[4,128]{1,0:T(4,128)}) custom-call(bf16[128,512]{1,0:T(8,128)(2,1)S(1)} %get-tuple-element.12.grad, f32[4,4,128]{2,1,0:T(4,128)S(1)} %get-tuple-element.13.par), custom_call_target="tpu_custom_call" | custom-call | tf_op jit(solution)/shard_map/finish/pallas_call | solution.py:712

commit v6 on v5

--- a/solution.py
+++ b/solution.py
@@ -194,30 +194,39 @@
     def at(y_of, z_of):
         return 4 * y_of + z_of
 
-    def relay(stage, kind, slot, target):
-        block = (cot.at[:, slot], quart.at[slot])[stage]
+    def relay(stage, kind, half, slot, target):
+        block = cot.at[half, slot] if stage == 0 else quart.at[slot, pl.ds(16 * half, 16)]
         return pltpu.make_async_remote_copy(
             src_ref=block,
             dst_ref=block,
             send_sem=send_relay.at[stage],
-            recv_sem=recv_relay.at[stage, kind],
+            recv_sem=recv_relay.at[stage, kind if kind == last else 2 * kind + half],
             device_id={"rows": target},
             device_id_type=MESH,
         )
 
     up, down, far = at(y_up, z), at(y_down, z), at(y_far, z)
-    last = 3
+    last = 6
 
     def gather_start(stage):
-        for kind, target in ((0, at(y, z_mate[1])), (last, up), (last, down), (1, at(y, z_mate[2])), (2, at(y, z_mate[3])), (last, far)):
-            relay(stage, kind, row, target).start()
+        for kind, target in (
+            (0, at(y, z_mate[1])),
+            (last, up),
+            (last, down),
+            (1, at(y, z_mate[2])),
+            (2, at(y, z_mate[3])),
+            (last, far),
+        ):
+            for half in range(2):
+                relay(stage, kind, half, row, target).start()
 
     def gather_relay(stage):
         for j in (1, 2, 3):
             slot = at(y, z_mate[j])
-            relay(stage, j - 1, slot, row).wait_recv()
-            for target in (far, up, down):
-                relay(stage, last, slot, target).start()
+            for half in range(2):
+                relay(stage, j - 1, half, slot, row).wait_recv()
+                for target in (far, up, down):
+                    relay(stage, last, half, slot, target).start()
 
     def gather_finish(stage):
         all_of((cot.at[:, pl.ds(0, 12)], quart.at[pl.ds(0, 12)])[stage], recv_relay.at[stage, last])
@@ -692,7 +701,7 @@
             dma((2, 2)),
             dma((4,)),
             dma((2,)),
-            dma((2, 4)),
+            dma((2, 7)),
             pltpu.SemaphoreType.REGULAR((2,)),
         ],
         compiler_params=pltpu.CompilerParams(collective_id=0, has_side_effects=True),

time: 51.6 us -> 51.6 us (level)
  no operation moved by 1% of the time
where the time goes in v6:
time: 51.6 us; the launch traced here: 51.5 us
  Pallas kernels  50.8 us (98%)
  between operations  0.64 us (1%)
    pallas_call x1, Pallas kernels, shards(): pl.pallas_call(functools.partial(kernel, sizes), out_shape=held, in_specs...  50.1 us

profile of v6, /device:TPU:1, one launch (start us, length us, event | category | flops | bytes accessed | tf_op | source)
XLA Modules:
  0.0 51.5 jit_solution(5009020033269130618)
XLA Ops:
  0.6 50.1 %levels.1 = (bf16[128,512]{1,0:T(8,128)(2,1)S(1)}, f32[4,4,128]{2,1,0:T(4,128)S(1)}) custom-call(bf16[128,512]{1,0:T(8,128)(2,1)} %bitcast.16, bf16[32,512]{1,0:T(8,128)(2,1)} %bitcast.17, bf16[2,16,512]{2,1,0:T(8,128)(2,1)} %bitcast.18, f32[1,512]{1,0:T(1,128)} %bitcast.19, f32[1,512]{1,0:T(1,128)} %bitcast.20, f32[1,512]{1,0:T(1,128)} %bitcast.21, ...), custom_call_target="tpu_custom_call" | custom-call | tf_op jit(solution)/shard_map/levels/pallas_call | solution.py:661
  50.8 0.7 %finish.1 = (bf16[128,512]{1,0:T(8,128)(2,1)}, f32[4,128]{1,0:T(4,128)}, f32[4,128]{1,0:T(4,128)}, f32[4,128]{1,0:T(4,128)}, f32[4,128]{1,0:T(4,128)}) custom-call(bf16[128,512]{1,0:T(8,128)(2,1)S(1)} %get-tuple-element.12.grad, f32[4,4,128]{2,1,0:T(4,128)S(1)} %get-tuple-element.13.par), custom_call_target="tpu_custom_call" | custom-call | tf_op jit(solution)/shard_map/finish/pallas_call | solution.py:721
